TPU v7x, 256 devices: a whole 4x4x8 slice. The times are simulated.
256 devices in a mesh: rep: 2 (over core), req: 32 (over y, z), tp: 4 (over x).
Axes of the slice: x: 4, y: 4, z: 8, core: 2. Of those that a mesh axis runs over, the one named last changes fastest.
Arguments:
- hidden: bfloat16 [1024, 1536], P(('rep', 'req'), 'tp'), may hold values from -6 to 6
- lengths: int32 [2, 512], P(None, 'req'), may hold values from 16 to 1024, as said below
- migrate: int32 [32], P('req'), may hold values from 0 to 15
- kv_cache: bfloat16 [1024, 1024, 8, 128], P(('rep', 'req'), None, 'tp'), may hold values from -250 to 250
- attn_gain: float32 [1536], replicated, may hold values from 0.1 to 1.9
- moe_gain: float32 [1536], replicated, may hold values from 0.1 to 1.9
- w_query: bfloat16 [1536, 1536], P(None, 'tp'), may hold values from -0.15625 to 0.15625
- key_value_weight: bfloat16 [1536, 1024], P(None, 'tp'), may hold values from -0.15625 to 0.15625
- output_weight: bfloat16 [1536, 1536], P('tp'), may hold values from -0.25 to 0.25
- w_gateup: bfloat16 [64, 1536, 2, 512], P(('rep', 'req'), None, None, 'tp'), may hold values from -0.15625 to 0.15625
- w_down: bfloat16 [64, 512, 1536], P(('rep', 'req'), 'tp'), may hold values from -0.25 to 0.25
- expert_ids: int32 [1024, 8], P(('rep', 'req')), may hold values from 0 to 63, all different within a row; in each aligned block of 16 rows (0 to 15, 16 to 31, ...) at most 6 rows name the same one
- expert_gates: float32 [1024, 8], P(('rep', 'req')), may hold values from 0.1 to 0.4
Outputs:
- layer_out: bfloat16 [1024, 1536], P(('rep', 'req'), 'tp')
Inputs may be any that keep to these rules, and one draw needn't show every extreme that they name: A request attends to its first lengths positions and to its own new key. `expert_ids`: each row names 8 distinct experts; among the rows of one device (an aligned block of 16 rows) no expert is named more than 6 times, and in some blocks one expert is named exactly 6 times.
All inputs are finite; a program needn't handle non-finite values.
Results may differ from a plain program's by a relative error of at most 0.015.
Values may be sent and summed in bfloat16 or wider, within the bound.
A program may use at most 64 MiB of HBM per device.

v0:
```python
import jax
import jax.numpy as jnp
from jax import lax
from jax.sharding import PartitionSpec as P

HEAD_SIZE = 64


epsilon = 1e-06
rope_base = 10000.0
masked_score = -1e30


def swapped(value, axis, apart):
    return lax.ppermute(value, axis, [(i, i ^ 1 << apart) for i in range(lax.axis_size(axis))])


def rms_norm(values, gain):
    mean_square = jnp.mean(values * values, axis=-1, keepdims=True)
    return values * lax.rsqrt(mean_square + epsilon) * gain


def apply_rotation(values, position):
    half_width = values.shape[-1] // 2
    inv_freq = rope_base ** (-jnp.arange(half_width, dtype=jnp.float32) * 2.0 / values.shape[-1])
    angles = position.astype(jnp.float32)[:, None, None] * inv_freq
    cosine = jnp.cos(angles)
    sine_part = jnp.sin(angles)
    first_half = values[..., :half_width]
    second_half = values[..., half_width:]
    return jnp.concatenate(
        [
            first_half * cosine - second_half * sine_part,
            second_half * cosine + first_half * sine_part,
        ],
        axis=-1,
    )


def attention(
    token_part, kv_rows, request_extent, attn_gain, w_query, key_value_weight, output_weight
):
    tokens = lax.all_gather(token_part, "tp", axis=1, tiled=True)
    row_count = tokens.shape[0]
    head_dim = HEAD_SIZE
    local_kv = kv_rows.shape[2]
    local_query = w_query.shape[1] // head_dim
    group_size = local_query // local_kv
    normalized_input = rms_norm(tokens.astype(jnp.float32), attn_gain).astype(jnp.bfloat16)
    query_vectors = jnp.dot(normalized_input, w_query, preferred_element_type=jnp.float32).reshape(
        row_count, local_query, head_dim
    )
    key_value_rows = jnp.dot(
        normalized_input, key_value_weight, preferred_element_type=jnp.float32
    ).reshape(row_count, local_kv, 2 * head_dim)
    query_vectors = (
        apply_rotation(query_vectors, request_extent)
        .astype(jnp.bfloat16)
        .reshape(row_count, local_kv, group_size, head_dim)
    )
    key_new = apply_rotation(key_value_rows[..., :head_dim], request_extent).astype(jnp.bfloat16)
    value_new = key_value_rows[..., head_dim:].astype(jnp.bfloat16)
    score_scale = head_dim ** (-0.5)
    cache_keys = kv_rows[..., :head_dim]
    cache_values = kv_rows[..., head_dim:]
    scores = (
        jnp.einsum("rhgd,rthd->rhgt", query_vectors, cache_keys, preferred_element_type=jnp.float32)
        * score_scale
    )
    own_score = (
        jnp.einsum("rhgd,rhd->rhg", query_vectors, key_new, preferred_element_type=jnp.float32)
        * score_scale
    )
    positions = jnp.arange(kv_rows.shape[1], dtype=jnp.int32)
    visible = positions[None, None, None, :] < request_extent[:, None, None, None]
    scores = jnp.where(visible, scores, masked_score)
    row_peak = jnp.maximum(jnp.max(scores, axis=-1), own_score)
    cache_prob = jnp.exp(scores - row_peak[..., None])
    own_prob = jnp.exp(own_score - row_peak)
    denominator = jnp.sum(cache_prob, axis=-1) + own_prob
    cache_weight = (cache_prob / denominator[..., None]).astype(jnp.bfloat16)
    own_weight = (own_prob / denominator).astype(jnp.bfloat16)
    mixture = jnp.einsum(
        "rhgt,rthd->rhgd", cache_weight, cache_values, preferred_element_type=jnp.float32
    )
    mixture = (
        mixture
        + own_weight.astype(jnp.float32)[..., None] * value_new.astype(jnp.float32)[:, :, None, :]
    )
    context = mixture.reshape(row_count, local_query * head_dim).astype(jnp.bfloat16)
    partial_out = jnp.dot(context, output_weight, preferred_element_type=jnp.float32)
    return tokens.astype(jnp.float32) + lax.psum(partial_out.astype(jnp.bfloat16), "tp").astype(
        jnp.float32
    )


def shards(
    hidden,
    lengths,
    migrate,
    kv_cache,
    attn_gain,
    moe_gain,
    w_query,
    key_value_weight,
    output_weight,
    w_gateup,
    w_down,
    expert_ids,
    expert_gates,
):
    row_count = hidden.shape[0]
    replica = lax.axis_index("rep")
    slot_index = jnp.arange(row_count, dtype=jnp.int32)
    chosen_slot = migrate[0]
    is_moved = slot_index == chosen_slot
    own_span = lax.dynamic_index_in_dim(lengths, replica, 0, keepdims=False)
    other_span = lax.dynamic_index_in_dim(lengths, 1 - replica, 0, keepdims=False)
    picked_cache = lax.dynamic_slice_in_dim(kv_cache, chosen_slot, 1, 0)
    picked_row = lax.dynamic_slice_in_dim(hidden, chosen_slot, 1, 0)
    cache_width = picked_cache.size
    packed = jnp.concatenate([picked_cache.reshape(1, cache_width), picked_row], axis=1)
    arrived = swapped(packed, "rep", 0)
    moved_cache = arrived[:, :cache_width].reshape(picked_cache.shape)
    moved_row = arrived[:, cache_width:]
    served_cache = lax.dynamic_update_slice_in_dim(kv_cache, moved_cache, chosen_slot, 0)
    served_rows = lax.dynamic_update_slice_in_dim(hidden, moved_row, chosen_slot, 0)
    request_extent = jnp.where(is_moved, other_span, own_span)
    residual = attention(
        served_rows,
        served_cache,
        request_extent,
        attn_gain,
        w_query,
        key_value_weight,
        output_weight,
    )
    full_width = moe_gain.shape[0]
    quarter = full_width // lax.axis_size("tp")
    expert_in = rms_norm(residual, moe_gain).astype(jnp.bfloat16)
    own_residual = lax.dynamic_slice_in_dim(residual, lax.axis_index("tp") * quarter, quarter, 1)
    expert_count = lax.axis_size("rep") * lax.axis_size("req")
    top_count = expert_ids.shape[1]
    capacity = min(row_count, max(3, 3 * row_count * top_count // expert_count))
    flat_ids = expert_ids.reshape(-1)
    matches = (flat_ids[:, None] == jnp.arange(expert_count, dtype=jnp.int32)[None, :]).astype(
        jnp.int32
    )
    slot_rank = jnp.sum((jnp.cumsum(matches, axis=0) - matches) * matches, axis=1)
    slot_target = flat_ids * capacity + slot_rank
    slot_table = (
        slot_target[:, None] == jnp.arange(expert_count * capacity, dtype=jnp.int32)[None, :]
    ).astype(jnp.float32)
    route_table = slot_table.reshape(row_count, top_count, -1).sum(axis=1)
    gate_table = (
        (slot_table * expert_gates.reshape(-1, 1)).reshape(row_count, top_count, -1).sum(axis=1)
    )
    outbound = jnp.einsum(
        "rs,rd->sd", route_table.astype(jnp.bfloat16), expert_in, preferred_element_type=jnp.float32
    ).astype(jnp.bfloat16)
    outbound = outbound.reshape(expert_count, capacity, -1)
    gate_up = w_gateup[0].reshape(w_gateup.shape[1], -1)
    down_rows = w_down[0]
    arrived_rows = lax.all_to_all(outbound, ("rep", "req"), split_axis=0, concat_axis=0, tiled=True)
    model_width = arrived_rows.shape[2]
    flattened = arrived_rows.reshape(-1, model_width)
    projected = jnp.dot(flattened, gate_up, preferred_element_type=jnp.float32)
    split_at = projected.shape[1] // 2
    activation = (jax.nn.silu(projected[:, :split_at]) * projected[:, split_at:]).astype(
        jnp.bfloat16
    )
    expert_part = jnp.dot(activation, down_rows, preferred_element_type=jnp.float32)
    expert_part = expert_part.reshape(arrived_rows.shape[0], arrived_rows.shape[1], model_width)
    returned = lax.all_to_all(
        expert_part.astype(jnp.bfloat16), ("rep", "req"), split_axis=0, concat_axis=0, tiled=True
    ).astype(expert_part.dtype)
    returned_rows = returned.reshape(expert_count * capacity, -1)
    combined = jnp.dot(
        gate_table,
        returned_rows,
        precision=lax.Precision.HIGHEST,
        preferred_element_type=jnp.float32,
    )
    expert_mix = lax.psum_scatter(
        combined.astype(jnp.bfloat16), "tp", scatter_dimension=1, tiled=True
    ).astype(jnp.float32)
    return (own_residual + expert_mix).astype(jnp.bfloat16)


def solution(mesh):
    placed = (
        P(("rep", "req"), "tp"),
        P(None, "req"),
        P("req"),
        P(("rep", "req"), None, "tp", None),
        P(),
        P(),
        P(None, "tp"),
        P(None, "tp"),
        P("tp", None),
        P(("rep", "req"), None, None, "tp"),
        P(("rep", "req"), "tp", None),
        P(("rep", "req"), None),
        P(("rep", "req"), None),
    )
    return jax.shard_map(
        shards, mesh=mesh, in_specs=placed, out_specs=P(("rep", "req"), "tp"), check_vma=False
    )
```

profile of v0, /device:TPU:8, one launch (start us, length us, event | category | flops | bytes accessed | tf_op | source)
XLA Modules:
  0.0 226.3 jit_solution(14845780851035790938)
XLA Ops:
  6.5 0.8 copy.69
  8.0 1.4 constant_dynamic-slice_fusion.3
  9.6 4.4 %pad_maximum_fusion = bf16[1,262528]{1,0:T(2,128)(2,1)S(1)} fusion(bf16[1,384]{1,0:T(2,128)(2,1)S(1)} %constant_dynamic-slice_fusion.2, bf16[1,262144]{1,0:T(2,128)(2,1)S(1)} %reshape.200), kind=kLoop, calls=%fused_computation.12 | loop fusion | flops 1050112 | bytes 1050112 | tf_op jit(solution)/shard_map/concatenate | solution.py:122
  14.2 21.2 %copy.45 = bf16[16,1024,2,128]{1,3,2,0:T(8,128)(2,1)} copy(bf16[16,1024,2,128]{3,2,1,0:T(2,128)(2,1)} %param.16) | data formatting | bytes 16777216 | tf_op args[3]
  36.6 1.0 copy-done.2
  37.7 12.2 %all_gather.3 = bf16[16,1536]{1,0:T(8,128)(2,1)S(1)} all-gather(bf16[16,384]{1,0:T(8,128)(2,1)S(1)} %dynamic_update_slice.6), channel_id=1, replica_groups=mesh['rep'=2,'req'=32,'tp'=4] {'tp'}, dimensions={1}, use_global_device_ids=true | all-gather | bytes 61440 | tf_op jit(solution)/shard_map/all_gather | solution.py:43
  49.9 9.9 %slice_reduce_fusion = bf16[262144]{0:T(1024)(128)(2,1)S(1)} fusion(bf16[1,262528]{1,0:T(2,128)(2,1)} %copy-done.2), kind=kLoop, calls=%fused_computation.13 | loop fusion | bytes 1048576 | tf_op jit(solution)/shard_map/slice | solution.py:124
  60.8 1.4 fusion.34
  62.5 0.9 constant_dynamic-update-slice_fusion
  63.7 3.0 %fusion.44 = (f32[16,2,3]{2,1,0:T(2,128)S(1)}, f32[16,2,3,1024]{3,2,1,0:T(4,128)S(1)}) fusion(bf16[16,1024,2,128]{1,3,2,0:T(8,128)(2,1)} %constant_dynamic-update-slice_fusion, bf16[16,2,3,32]{3,2,1,0:T(4,128)(2,1)S(1)} %copy.44, bf16[16,2,3,32]{3,2,1,0:T(4,128)(2,1)S(1)} %copy.43, pred[16,1024]{1,0:T(8,128)(4,1)S(1)} %iota_compare_fusion.2), kind=kOutput, calls=%fused_computation.77 | convolution fusion | flops 12902304 | bytes 4616576 | tf_op jit(solution)/shard_map/rhgd,rthd->rhgt/dot_general | solution.py:67
  67.2 3.5 %fusion.13 = bf16[16,2,3,64]{3,2,1,0:T(4,128)(2,1)S(1)} fusion(bf16[16,1024,2,128]{1,3,2,0:T(8,128)(2,1)} %constant_dynamic-update-slice_fusion, f32[16,2,3,1024]{3,2,1,0:T(4,128)S(1)} %get-tuple-element.20, f32[16,2,3]{2,1,0:T(2,128)S(1)} %get-tuple-element.14, f32[16,2,3]{2,1,0:T(2,128)S(1)} %multiply_maximum_fusion, f32[16,2,64]{2,1,0:T(2,128)S(1)} %fusion.38, ...), kind=kOutput, calls=%fused_computation.11 | convolution fusion | flops 12896256 | bytes 4609152 | tf_op jit(solution)/shard_map/rhgt,rthd->rhgd/dot_general | solution.py:83
  71.0 17.0 %psum.7 = bf16[16,1536]{1,0:T(8,128)(2,1)S(1)} all-reduce(bf16[16,1536]{1,0:T(8,128)(2,1)S(1)} %convolution_convert_fusion.3), channel_id=1, replica_groups=mesh['rep'=2,'req'=32,'tp'=4] {'tp'}, use_global_device_ids=true, to_apply=%region_3.4 | all-reduce | flops 24576 | bytes 98304 | tf_op jit(solution)/shard_map/psum | solution.py:92
  88.2 1.5 convolution_convert_fusion
  89.7 2.2 reshape.204
  91.9 51.9 %all_to_all.10 = bf16[64,6,1536]{2,1,0:T(8,128)(2,1)} all-to-all(bf16[64,6,1536]{2,1,0:T(8,128)(2,1)S(1)} %reshape.204), channel_id=1, replica_groups=mesh['rep'=2,'req'=32,'tp'=4] {'rep','req'}, dimensions={0} | all-to-all | bytes 2359296 | tf_op jit(solution)/shard_map/all_to_all | solution.py:164
  143.8 2.3 %reshape.205 = bf16[384,1536]{1,0:T(8,128)(2,1)S(1)} reshape(bf16[64,6,1536]{2,1,0:T(8,128)(2,1)} %all_to_all.10) | data formatting | bytes 2359296 | tf_op jit(solution)/shard_map/reshape | solution.py:166
  146.1 1.7 fusion.16
  148.4 0.7 copy.51
  149.0 45.9 %all_to_all.11 = bf16[64,6,1536]{2,1,0:T(8,128)(2,1)S(1)} all-to-all(bf16[64,6,1536]{2,1,0:T(8,128)(2,1)S(1)} %copy.51), channel_id=1, replica_groups=mesh['rep'=2,'req'=32,'tp'=4] {'rep','req'}, dimensions={0} | all-to-all | bytes 2359296 | tf_op jit(solution)/shard_map/all_to_all | solution.py:174
  195.0 1.2 reshape.206
  196.2 1.8 convolution_convert_fusion.2
  198.0 0.9 copy.54
  199.0 18.9 %reduce-scatter.4.cloned.1.call-done = bf16[384,16]{1,0:T(8,128)(2,1)} async-done(((bf16[1536,16]{1,0:T(8,128)(2,1)}), bf16[384,16]{1,0:T(8,128)(2,1)}) %reduce-scatter.4.cloned.1.call-update) | async-done | bytes 12304
  217.9 1.0 copy.55
  (64 shorter events, 5.2 us)
Async XLA Ops:
  6.5 64.2 %copy-start = (bf16[384,1536]{1,0:T(8,128)(2,1)S(1)}, bf16[384,1536]{1,0:T(8,128)(2,1)}, u32[]{:S(2)}) copy-start(bf16[384,1536]{1,0:T(8,128)(2,1)} %param.21) | copy-start | bytes 3538948
  6.5 211.4 %reduce-scatter.4.cloned.1.call-start = ((), (), s32[]{:S(2)}) async-start(), calls=%async_computation.3 | async-start | bytes 491520
  14.0 21.3 %copy-start.6 = (s32[16,8]{0,1:T(8,128)S(1)}, s32[16,8]{0,1:T(8,128)}, u32[]{:S(2)}) copy-start(s32[16,8]{0,1:T(8,128)} %param.24) | copy-start | bytes 1540
  14.1 22.0 %copy-start.7 = (f32[16,8]{0,1:T(8,128)S(1)}, f32[16,8]{0,1:T(8,128)}, u32[]{:S(2)}) copy-start(f32[16,8]{0,1:T(8,128)} %param.25) | copy-start | bytes 1540
  14.1 22.3 %copy-start.8 = (s32[2,16]{1,0:T(2,128)S(1)}, s32[2,16]{1,0:T(2,128)}, u32[]{:S(2)}) copy-start(s32[2,16]{1,0:T(2,128)} %param.14) | copy-start | bytes 388
  14.1 22.5 %collective-permute-start = (bf16[1,262528]{1,0:T(2,128)(2,1)S(1)}, bf16[1,262528]{1,0:T(2,128)(2,1)S(1)}, u32[]{:S(2)}, u32[]{:S(2)}) collective-permute-start(bf16[1,262528]{1,0:T(2,128)(2,1)S(1)} %pad_maximum_fusion), channel_id=1, source_target_pairs={{0,128},{128,0},{1,129},{129,1},{2,130},{130,2},{3,131},{131,3},{4... | collective-permute-start | bytes 1575176 | tf_op jit(solution)/shard_map/ppermute | solution.py:15
  36.6 1.1 copy-start.2
  49.9 10.4 %copy-start.1 = (bf16[1536,384]{1,0:T(8,128)(2,1)S(1)}, bf16[1536,384]{1,0:T(8,128)(2,1)}, u32[]{:S(2)}) copy-start(bf16[1536,384]{1,0:T(8,128)(2,1)} %param.19) | copy-start | bytes 3538948
  49.9 10.4 %copy-start.4 = (f32[1536]{0:T(1024)S(1)}, f32[1536]{0:T(1024)}, u32[]{:S(2)}) copy-start(f32[1536]{0:T(1024)} %param.17) | copy-start | bytes 18436
  70.6 17.6 %copy-start.5 = (f32[1536]{0:T(1024)S(1)}, f32[1536]{0:T(1024)}, u32[]{:S(2)}) copy-start(f32[1536]{0:T(1024)} %param.18) | copy-start | bytes 18436
  146.1 1.8 copy-start.3
Sparse Core Ops, SparseCore 0:
  199.1 18.7 reduce-scatter.3
where the time goes:
time: 227 us; the launch traced here: 226 us
  blocking collectives  127 us (56%)
  local copies, waits for them, and re-layouts  44.7 us (20%)
  waiting for transfers between devices  18.9 us (8%)
  between operations  14.4 us (6%)
  matrix products  14.1 us (6%)
  other arithmetic  6.97 us (3%)
    all_to_all x1, blocking collectives, shards(): lax.all_to_all(outbound, ('rep', 'req'), split_axis=0, concat_axis=0, til...  51.9 us
    all_to_all x1, blocking collectives, shards(): lax.all_to_all(expert_part.astype(jnp.bfloat16), ('rep', 'req'), split_ax...  45.9 us
    unnamed x24, local copies, waits for them, and re-layouts  25.1 us
    unnamed x2, waiting for transfers between devices  18.9 us
    psum x1, blocking collectives, attention(): lax.psum(partial_out.astype(jnp.bfloat16), 'tp').astype(jnp.float32)  17 us
    all_gather x1, blocking collectives, attention(): tokens = lax.all_gather(token_part, 'tp', axis=1, tiled=True)  12.2 us
    slice x1, local copies, waits for them, and re-layouts, shards(): moved_cache = arrived[:, :cache_width].reshape(picked_cache.shape)  9.86 us
  transfers between devices with their start and end apart: 2, of which 1 were waited for; matrix products, arithmetic and copies ran while one was open for 10% of the time, Pallas kernels for 0%

commit v1 on v0

v1 whole, which is shorter than its diff:
```python
import functools
import jax
import jax.numpy as jnp
import numpy as np
from jax import lax
from jax.experimental import pallas as pl
from jax.experimental.pallas import tpu as pltpu
from jax.sharding import PartitionSpec as P

MESH = pl.DeviceIdType.MESH
HEAD_SIZE = 64
EPSILON = 1e-06
ROPE_BASE = 10000.0
MASKED = -1e30
GATE_LANES = 128


def rows_of(scalars, n):
    row = lax.broadcasted_iota(jnp.int32, (n, 128), 0)
    out = jnp.zeros((n, 128), jnp.int32)
    for r in range(n):
        out = jnp.where(row == r, scalars(r), out)
    return out


def attend(q, kvn, kv, bias, limit):
    scale = HEAD_SIZE ** (-0.5)
    s = lax.dot_general(q.astype(jnp.bfloat16), kv, (((1,), (1,)), ((), ())), preferred_element_type=jnp.float32)
    lane = lax.broadcasted_iota(jnp.int32, s.shape, 1)
    s = jnp.where(lane < limit, s * scale + bias, MASKED)
    own = jnp.sum(q * kvn, axis=1, keepdims=True) * scale
    peak = jnp.maximum(jnp.max(s, axis=1, keepdims=True), own)
    p = jnp.exp(s - peak)
    p_own = jnp.exp(own - peak)
    inv = 1.0 / (jnp.sum(p, axis=1, keepdims=True) + p_own)
    w = (p * inv).astype(jnp.bfloat16)
    w_own = (p_own * inv).astype(jnp.bfloat16).astype(jnp.float32)
    return jnp.dot(w, kv, preferred_element_type=jnp.float32) + w_own * kvn


def attention_kernel(
    n_tp,
    len_s, mig_s, hid, kv_h, ag, mg, freq, wq_h, wkv_h, wo_h, ids, gates,
    x_out, res_out,
    kv_v, wq_v, wkv_v, wo_v, tok, kv_send, kv_recv, part_send, part_recv, q_s, kvn_s, ctx_s, bias_s,
    load_sem, kv_sem, tok_send_sem, tok_recv_sem, kv_send_sem, kv_recv_sem, part_send_sem, part_recv_sem,
):
    rep, tp = lax.axis_index("rep"), lax.axis_index("tp")
    n, width = hid.shape
    model = n_tp * width
    heads = wq_v.shape[1] // HEAD_SIZE
    kvh = wkv_v.shape[1] // (2 * HEAD_SIZE)
    group = heads // kvh
    n_lanes = kv_v.shape[1]

    loads = []
    for i, (src, dst) in enumerate(((wq_h, wq_v), (wkv_h, wkv_v))):
        loads.append(pltpu.make_async_copy(src, dst, load_sem.at[i]))
    load_o = pltpu.make_async_copy(wo_h, wo_v, load_sem.at[2])
    for c in loads:
        c.start()
    kv_loads = [pltpu.make_async_copy(kv_h.at[r], kv_v.at[r], kv_sem.at[r]) for r in range(n)]
    for c in kv_loads:
        c.start()
    load_o.start()

    barrier = pltpu.get_barrier_semaphore()
    peers = []
    for k in range(1, n_tp):
        peers.append((0, lax.rem(tp + k, n_tp)))
    for k in range(n_tp):
        peers.append((1, lax.rem(tp + k, n_tp)))
    for side, t in peers:
        r = rep if side == 0 else 1 - rep
        pl.semaphore_signal(barrier, inc=1, device_id={"rep": r, "tp": t}, device_id_type=MESH)
    pl.semaphore_wait(barrier, len(peers))

    sends = []
    for i, (side, t) in enumerate(peers):
        r = rep if side == 0 else 1 - rep
        c = pltpu.make_async_remote_copy(
            src_ref=hid, dst_ref=tok.at[side, tp], send_sem=tok_send_sem.at[i],
            recv_sem=tok_recv_sem.at[side, tp], device_id={"rep": r, "tp": t}, device_id_type=MESH)
        c.start()
        sends.append(c)
    tok[0, tp] = hid[...]

    slot = mig_s[0]
    row = lax.broadcasted_iota(jnp.int32, (n, 128), 0)
    lane = lax.broadcasted_iota(jnp.int32, (n, 128), 1)
    moved = row == slot
    own_span = rows_of(lambda r: jnp.where(rep == 0, len_s[0, r], len_s[1, r]), n)
    other_span = rows_of(lambda r: jnp.where(rep == 0, len_s[1, r], len_s[0, r]), n)
    span = jnp.where(moved, other_span, own_span).astype(jnp.float32)
    angle = span * freq[...]
    cosine, sine = jnp.cos(angle), jnp.sin(angle)
    first = lax.rem(lane, HEAD_SIZE) < HEAD_SIZE // 2
    half = HEAD_SIZE // 2

    def rotate(v):
        turned = jnp.where(first, -pltpu.roll(v, 128 - half, 1), pltpu.roll(v, half, 1))
        return v * cosine + turned * sine

    head = lax.broadcasted_iota(jnp.int32, (8, n_lanes), 0)
    pos = lax.broadcasted_iota(jnp.int32, (8, n_lanes), 1)
    bias_s[...] = jnp.where(lax.rem(pos, kvh) == head // group, 0.0, MASKED)

    eye = row == lane
    expert = lax.rem(lane, GATE_LANES // 2)
    dense = jnp.zeros((n, 128), jnp.float32)
    for k in range(ids.shape[0]):
        idc = jnp.sum(jnp.where(eye, ids[k:k + 1, :], 0), axis=1, keepdims=True)
        gc = jnp.sum(jnp.where(eye, gates[k:k + 1, :], 0.0), axis=1, keepdims=True)
        dense = dense + jnp.where(expert == idc, gc, 0.0)
    high = dense.astype(jnp.bfloat16)
    low = (dense - high.astype(jnp.float32)).astype(jnp.bfloat16)
    x_out[:, 0:GATE_LANES] = jnp.where(lane < GATE_LANES // 2, high.astype(jnp.float32), low.astype(jnp.float32)).astype(jnp.bfloat16)

    for side, t in peers:
        pltpu.make_async_remote_copy(
            src_ref=hid, dst_ref=tok.at[side, t], send_sem=tok_send_sem.at[0],
            recv_sem=tok_recv_sem.at[side, t], device_id={"tp": t}, device_id_type=MESH).wait_recv()
    for c in sends:
        c.wait_send()

    moved_w = lax.broadcasted_iota(jnp.int32, (n, width), 0) == slot
    tokens = jnp.concatenate(
        [jnp.where(moved_w, tok[1, t].astype(jnp.float32), tok[0, t].astype(jnp.float32)) for t in range(n_tp)], axis=1)
    mean = jnp.mean(tokens * tokens, axis=1, keepdims=True)
    normed = (tokens * lax.rsqrt(mean + EPSILON) * ag[...]).astype(jnp.bfloat16)
    for c in loads:
        c.wait()
    queries = jnp.dot(normed, wq_v[...], preferred_element_type=jnp.float32)
    keyval = jnp.dot(normed, wkv_v[...], preferred_element_type=jnp.float32)
    q_s[...] = jnp.zeros_like(q_s)
    kvn_s[...] = jnp.zeros_like(kvn_s)
    low_lanes = lane < HEAD_SIZE
    for b in range(heads // 2):
        turned = rotate(queries[:, b * 128:(b + 1) * 128]).astype(jnp.bfloat16).astype(jnp.float32)
        q_s[:, 2 * b, :] = jnp.where(low_lanes, turned, 0.0)
        q_s[:, 2 * b + 1, :] = jnp.where(low_lanes, pltpu.roll(turned, HEAD_SIZE, 1), 0.0)
    for g in range(kvh):
        both = keyval[:, g * 128:(g + 1) * 128]
        both = jnp.where(low_lanes, rotate(both), both).astype(jnp.bfloat16).astype(jnp.float32)
        for h in range(g * group, (g + 1) * group):
            kvn_s[:, h, :] = both

    for c in kv_loads:
        c.wait()
    kv_send[...] = kv_v[slot]
    kv_copy = pltpu.make_async_remote_copy(
        src_ref=kv_send, dst_ref=kv_recv, send_sem=kv_send_sem, recv_sem=kv_recv_sem,
        device_id={"rep": 1 - rep}, device_id_type=MESH)
    kv_copy.start()

    def one(r):
        limit = kvh * jnp.where(rep == 0, len_s[0, r], len_s[1, r])
        ctx_s[r] = attend(q_s[r], kvn_s[r], kv_v[r], bias_s[...], limit)

    UNROLL = 4

    def step(i, carry):
        for j in range(UNROLL):
            one(i * UNROLL + j)
        return carry

    lax.fori_loop(0, n // UNROLL, step, 0)
    kv_copy.wait()
    limit = kvh * jnp.where(rep == 0, len_s[1, slot], len_s[0, slot])
    arrived = attend(q_s[slot], kvn_s[slot], kv_recv[...], bias_s[...], limit)

    blocks = []
    for b in range(heads // 2):
        even = jnp.where(moved, arrived[2 * b:2 * b + 1], ctx_s[:, 2 * b, :])
        odd = jnp.where(moved, arrived[2 * b + 1:2 * b + 2], ctx_s[:, 2 * b + 1, :])
        blocks.append(jnp.where(low_lanes, pltpu.roll(even, HEAD_SIZE, 1), odd))
    context = jnp.concatenate(blocks, axis=1).astype(jnp.bfloat16)
    load_o.wait()
    partial = jnp.dot(context, wo_v[...], preferred_element_type=jnp.float32)
    part_send[...] = partial.astype(jnp.bfloat16)
    sends = []
    for k in range(1, n_tp):
        t = lax.rem(tp + k, n_tp)
        c = pltpu.make_async_remote_copy(
            src_ref=part_send, dst_ref=part_recv.at[tp], send_sem=part_send_sem.at[k],
            recv_sem=part_recv_sem.at[tp], device_id={"tp": t}, device_id_type=MESH)
        c.start()
        sends.append(c)
    total = tokens + part_send[...].astype(jnp.float32)
    for k in range(1, n_tp):
        t = lax.rem(tp + k, n_tp)
        pltpu.make_async_remote_copy(
            src_ref=part_send, dst_ref=part_recv.at[t], send_sem=part_send_sem.at[k],
            recv_sem=part_recv_sem.at[t], device_id={"tp": t}, device_id_type=MESH).wait_recv()
        total = total + part_recv[t].astype(jnp.float32)
    mean = jnp.mean(total * total, axis=1, keepdims=True)
    x_out[:, GATE_LANES:] = (total * lax.rsqrt(mean + EPSILON) * mg[...]).astype(jnp.bfloat16)
    mine = jnp.zeros((n, width), jnp.float32)
    for t in range(n_tp):
        mine = jnp.where(tp == t, total[:, t * width:(t + 1) * width], mine)
    res_out[...] = mine
    for c in sends:
        c.wait_send()


def attention(n_tp, lengths, migrate, hidden, kv_cache, attn_gain, moe_gain, w_query, key_value_weight, output_weight, expert_ids, expert_gates):
    n, width = hidden.shape
    model = w_query.shape[0]
    kvh = kv_cache.shape[2]
    kv = kv_cache.reshape(n, kv_cache.shape[1] * kvh, kv_cache.shape[3])
    lanes = kv.shape[1]
    i = np.arange(128) % (HEAD_SIZE // 2)
    freq = jnp.asarray((ROPE_BASE ** (-2.0 * i / HEAD_SIZE)).astype(np.float32)[None])
    ids = jnp.pad(expert_ids.T, ((0, 0), (0, 128 - n)))
    gates = jnp.pad(expert_gates.T, ((0, 0), (0, 128 - n)))
    smem, vmem, hbm = (pl.BlockSpec(memory_space=s) for s in (pltpu.SMEM, pltpu.VMEM, pl.ANY))
    bf, f32 = jnp.bfloat16, jnp.float32
    dma = pltpu.SemaphoreType.DMA
    return pl.pallas_call(
        functools.partial(attention_kernel, n_tp),
        name="attention",
        out_shape=(jax.ShapeDtypeStruct((n, GATE_LANES + model), bf), jax.ShapeDtypeStruct((n, width), f32)),
        in_specs=[smem, smem, vmem, hbm, vmem, vmem, vmem, hbm, hbm, hbm, vmem, vmem],
        out_specs=(vmem, vmem),
        scratch_shapes=[
            pltpu.VMEM(kv.shape, bf),
            pltpu.VMEM(w_query.shape, bf), pltpu.VMEM(key_value_weight.shape, bf), pltpu.VMEM(output_weight.shape, bf),
            pltpu.VMEM((2, n_tp, n, width), bf),
            pltpu.VMEM(kv.shape[1:], bf), pltpu.VMEM(kv.shape[1:], bf),
            pltpu.VMEM((n, model), bf), pltpu.VMEM((n_tp, n, model), bf),
            pltpu.VMEM((n, 8, 128), f32), pltpu.VMEM((n, 8, 128), f32), pltpu.VMEM((n, 8, 128), f32),
            pltpu.VMEM((8, lanes), f32),
            dma((3,)), dma((n,)), dma((2 * n_tp,)), dma((2, n_tp)), dma, dma, dma((n_tp,)), dma((n_tp,)),
        ],
        compiler_params=pltpu.CompilerParams(collective_id=0, has_side_effects=True, vmem_limit_bytes=50 * 2**20),
        cost_estimate=pl.CostEstimate(flops=200_000_000, bytes_accessed=12_000_000, transcendentals=1_000_000),
    )(lengths, migrate, hidden, kv, attn_gain.reshape(1, -1), moe_gain.reshape(1, -1), freq, w_query, key_value_weight, output_weight, ids, gates)


def shards(
    hidden,
    lengths,
    migrate,
    kv_cache,
    attn_gain,
    moe_gain,
    w_query,
    key_value_weight,
    output_weight,
    w_gateup,
    w_down,
    expert_ids,
    expert_gates,
):
    row_count = hidden.shape[0]
    x, own_residual = attention(lax.axis_size('tp'), lengths, migrate, hidden, kv_cache, attn_gain, moe_gain, w_query, key_value_weight, output_weight, expert_ids, expert_gates)
    expert_in = x[:, GATE_LANES:]
    expert_count = lax.axis_size("rep") * lax.axis_size("req")
    top_count = expert_ids.shape[1]
    capacity = min(row_count, max(3, 3 * row_count * top_count // expert_count))
    flat_ids = expert_ids.reshape(-1)
    matches = (flat_ids[:, None] == jnp.arange(expert_count, dtype=jnp.int32)[None, :]).astype(
        jnp.int32
    )
    slot_rank = jnp.sum((jnp.cumsum(matches, axis=0) - matches) * matches, axis=1)
    slot_target = flat_ids * capacity + slot_rank
    slot_table = (
        slot_target[:, None] == jnp.arange(expert_count * capacity, dtype=jnp.int32)[None, :]
    ).astype(jnp.float32)
    route_table = slot_table.reshape(row_count, top_count, -1).sum(axis=1)
    gate_table = (
        (slot_table * expert_gates.reshape(-1, 1)).reshape(row_count, top_count, -1).sum(axis=1)
    )
    outbound = jnp.einsum(
        "rs,rd->sd", route_table.astype(jnp.bfloat16), expert_in, preferred_element_type=jnp.float32
    ).astype(jnp.bfloat16)
    outbound = outbound.reshape(expert_count, capacity, -1)
    gate_up = w_gateup[0].reshape(w_gateup.shape[1], -1)
    down_rows = w_down[0]
    arrived_rows = lax.all_to_all(outbound, ("rep", "req"), split_axis=0, concat_axis=0, tiled=True)
    model_width = arrived_rows.shape[2]
    flattened = arrived_rows.reshape(-1, model_width)
    projected = jnp.dot(flattened, gate_up, preferred_element_type=jnp.float32)
    split_at = projected.shape[1] // 2
    activation = (jax.nn.silu(projected[:, :split_at]) * projected[:, split_at:]).astype(
        jnp.bfloat16
    )
    expert_part = jnp.dot(activation, down_rows, preferred_element_type=jnp.float32)
    expert_part = expert_part.reshape(arrived_rows.shape[0], arrived_rows.shape[1], model_width)
    returned = lax.all_to_all(
        expert_part.astype(jnp.bfloat16), ("rep", "req"), split_axis=0, concat_axis=0, tiled=True
    ).astype(expert_part.dtype)
    returned_rows = returned.reshape(expert_count * capacity, -1)
    combined = jnp.dot(
        gate_table,
        returned_rows,
        precision=lax.Precision.HIGHEST,
        preferred_element_type=jnp.float32,
    )
    expert_mix = lax.psum_scatter(
        combined.astype(jnp.bfloat16), "tp", scatter_dimension=1, tiled=True
    ).astype(jnp.float32)
    return (own_residual + expert_mix).astype(jnp.bfloat16)


def solution(mesh):
    placed = (
        P(("rep", "req"), "tp"),
        P(None, "req"),
        P("req"),
        P(("rep", "req"), None, "tp", None),
        P(),
        P(),
        P(None, "tp"),
        P(None, "tp"),
        P("tp", None),
        P(("rep", "req"), None, None, "tp"),
        P(("rep", "req"), "tp", None),
        P(("rep", "req"), None),
        P(("rep", "req"), None),
    )
    return jax.shard_map(
        shards, mesh=mesh, in_specs=placed, out_specs=P(("rep", "req"), "tp"), check_vma=False
    )
```

time: 227 us -> 174 us (0.77)
  blocking collectives: 127 us -> 97.8 us
  local copies, waits for them, and re-layouts: 44.7 us -> 16 us
  Pallas kernels: 0 us -> 23.1 us
  matrix products: 14.1 us -> 1.97 us
  other arithmetic: 6.97 us -> 1.31 us
    pallas_call x0 -> x1, Pallas kernels: none -> 23.1 us  [attention(): pl.pallas_call(functools.partial(attention_kernel, n_tp), name='attention...]
    psum x1 -> x0, blocking collectives: 17 us -> none  [attention(): lax.psum(partial_out.astype(jnp.bfloat16), 'tp').astype(jnp.float32)]
    unnamed x24 -> x20, local copies, waits for them, and re-layouts: 25.1 us -> 9.12 us
    all_gather x1 -> x0, blocking collectives: 12.2 us -> none  [attention(): tokens = lax.all_gather(token_part, 'tp', axis=1, tiled=True)]
    slice x2 -> x0, local copies, waits for them, and re-layouts: 9.87 us -> none  [the longest x1 9.86 us: shards(): moved_cache = arrived[:, :cache_width].reshape(picked_cache.shape)]
    dot_general x6 -> x0, matrix products: 8.68 us -> none  [the longest x1 3.46 us: attention(): jnp.einsum('rhgt,rthd->rhgd', cache_weight, cache_values, preferred_eleme...]
    concatenate x2 -> x0, other arithmetic: 4.5 us -> none  [the longest x1 4.41 us: shards(): jnp.concatenate([picked_cache.reshape(1, cache_width), picked_row], axis=1)]
  transfers between devices with their start and end apart: 2 -> 1, of which waited for: 1 -> 1; matrix products, arithmetic and copies ran while one was open for 10% -> 0% of each run, Pallas kernels for 0% -> 0%
where the time goes in v1:
time: 174 us; the launch traced here: 173 us
  blocking collectives  97.8 us (56%)
  Pallas kernels  23.1 us (13%)
  waiting for transfers between devices  18.7 us (11%)
  local copies, waits for them, and re-layouts  16 us (9%)
  between operations  14.2 us (8%)
  matrix products  1.97 us (1%)
    all_to_all x1, blocking collectives, shards(): lax.all_to_all(outbound, ('rep', 'req'), split_axis=0, concat_axis=0, til...  51.9 us
    all_to_all x1, blocking collectives, shards(): lax.all_to_all(expert_part.astype(jnp.bfloat16), ('rep', 'req'), split_ax...  45.9 us
    pallas_call x1, Pallas kernels, attention(): pl.pallas_call(functools.partial(attention_kernel, n_tp), name='attention...  23.1 us
    unnamed x2, waiting for transfers between devices  18.7 us
    unnamed x20, local copies, waits for them, and re-layouts  9.12 us
  transfers between devices with their start and end apart: 1, of which 1 were waited for; matrix products, arithmetic and copies ran while one was open for 0% of the time, Pallas kernels for 0%

profile of v1, /device:TPU:8, one launch (start us, length us, event | category | flops | bytes accessed | tf_op | source)
XLA Modules:
  0.0 173.2 jit_solution(2647229366905755126)
XLA Ops:
  7.2 0.7 reshape.56.ag
  7.9 0.7 reshape.57.mg
  8.6 0.8 copy.29
  9.5 0.8 copy.31
  10.3 0.7 pad.8.ids
  11.5 0.7 pad.9.gates
  12.4 1.3 copy-done.1
  13.7 1.3 copy-done.2
  14.9 1.1 copy-done.3
  16.1 0.7 copy-done.4
  16.8 0.7 copy-done.5
  17.4 0.7 copy-done.6
  18.1 23.1 %attention.1 = (bf16[16,1664]{1,0:T(8,128)(2,1)S(1)}, f32[16,384]{1,0:T(8,128)S(1)}) custom-call(s32[2,16]{1,0:T(2,128)S(1)} %copy-done.5, s32[1]{0:T(128)S(6)} %copy.43.mig_s, bf16[16,384]{1,0:T(8,128)(2,1)S(1)} %copy-done.4, bf16[16,2048,128]{2,1,0:T(8,128)(2,1)} %bitcast.18, f32[1,1536]{1,0:T(1,128)S(1)} %reshape.56.ag, f32[1,1536]{1,0:T(1,128)S(1)} %reshape.57.mg, ...), custom_call_target="tpu_custom_call" | custom-call | flops 200000000 | bytes 12000000 | tf_op jit(solution)/shard_map/attention/pallas_call | solution.py:219
  41.2 0.5 convolution_convert_fusion
  42.2 51.9 %all_to_all.10 = bf16[64,6,1536]{2,1,0:T(8,128)(2,1)} all-to-all(bf16[64,6,1536]{2,1,0:T(8,128)(2,1)S(1)} %reshape.58), channel_id=1, replica_groups=mesh['rep'=2,'req'=32,'tp'=4] {'rep','req'}, dimensions={0} | all-to-all | bytes 2359296 | tf_op jit(solution)/shard_map/all_to_all | solution.py:280
  94.1 2.4 %reshape.59 = bf16[384,1536]{1,0:T(8,128)(2,1)S(1)} reshape(bf16[64,6,1536]{2,1,0:T(8,128)(2,1)} %all_to_all.10) | data formatting | bytes 2359296 | tf_op jit(solution)/shard_map/reshape | solution.py:282
  96.5 0.5 fusion
  97.5 0.7 copy.33
  98.2 45.9 %all_to_all.11 = bf16[64,6,1536]{2,1,0:T(8,128)(2,1)S(1)} all-to-all(bf16[64,6,1536]{2,1,0:T(8,128)(2,1)S(1)} %copy.33), channel_id=1, replica_groups=mesh['rep'=2,'req'=32,'tp'=4] {'rep','req'}, dimensions={0} | all-to-all | bytes 2359296 | tf_op jit(solution)/shard_map/all_to_all | solution.py:290
  144.6 0.6 convolution_convert_fusion.2
  145.1 0.9 copy.34
  146.1 18.7 %reduce-scatter.4.cloned.1.call-done = bf16[384,16]{1,0:T(8,128)(2,1)} async-done(((bf16[1536,16]{1,0:T(8,128)(2,1)}), bf16[384,16]{1,0:T(8,128)(2,1)}) %reduce-scatter.4.cloned.1.call-update) | async-done | bytes 12304
  164.8 1.0 copy.35
  165.8 0.6 add_convert_fusion
  (24 shorter events, 2.2 us)
Async XLA Ops:
  6.5 90.5 %copy-start = (bf16[1,128,1536]{2,1,0:T(8,128)(2,1)S(1)}, bf16[1,128,1536]{2,1,0:T(8,128)(2,1)}, u32[]{:S(2)}) copy-start(bf16[1,128,1536]{2,1,0:T(8,128)(2,1)} %param.24) | copy-start | bytes 1179652
  6.5 158.3 %reduce-scatter.4.cloned.1.call-start = ((), (), s32[]{:S(2)}) async-start(), calls=%async_computation.3 | async-start | bytes 491520
  12.4 1.3 copy-start.1
  13.7 1.3 copy-start.2
  14.9 1.1 copy-start.3
  16.1 0.7 copy-start.4
  16.8 0.7 copy-start.5
  17.4 0.7 copy-start.6
  94.1 2.4 %copy-start.7 = (bf16[1,1536,2,128]{3,2,1,0:T(2,128)(2,1)S(1)}, bf16[1,1536,2,128]{3,2,1,0:T(2,128)(2,1)}, u32[]{:S(2)}) copy-start(bf16[1,1536,2,128]{3,2,1,0:T(2,128)(2,1)} %param.23) | copy-start | bytes 2359300
Sparse Core Ops, SparseCore 0:
  146.2 18.5 reduce-scatter.3

commit v2 on v1

--- a/solution.py
+++ b/solution.py
@@ -232,9 +232,295 @@
             pltpu.VMEM((8, lanes), f32),
             dma((3,)), dma((n,)), dma((2 * n_tp,)), dma((2, n_tp)), dma, dma, dma((n_tp,)), dma((n_tp,)),
         ],
-        compiler_params=pltpu.CompilerParams(collective_id=0, has_side_effects=True, vmem_limit_bytes=50 * 2**20),
+        compiler_params=pltpu.CompilerParams(collective_id=0, has_side_effects=True, vmem_limit_bytes=67_000_000),
         cost_estimate=pl.CostEstimate(flops=200_000_000, bytes_accessed=12_000_000, transcendentals=1_000_000),
     )(lengths, migrate, hidden, kv, attn_gain.reshape(1, -1), moe_gain.reshape(1, -1), freq, w_query, key_value_weight, output_weight, ids, gates)
+
+
+NY, NZ = 4, 8
+
+
+def experts_kernel(
+    n_tp, n_req,
+    x, res, gu_h, dn_h,
+    out,
+    ga, gb, pa, pb, raw, wide, gu, dn,
+    by_s, by_r, sa, ra, sb, rb, ys, yr, xs, xr, xf,
+    load_sem, wx_s, wx_r, a1_s, a1_r, a2_s, a2_r, b1_s, b1_r, b2_s, b2_r,
+    rby_s, rby_r, rsa_s, rsa_r, rsb_s, rsb_r, ry_s, ry_r, rx_s, rx_r,
+):
+    rep, req, tp = lax.axis_index("rep"), lax.axis_index("req"), lax.axis_index("tp")
+    y, z = req // NZ, lax.rem(req, NZ)
+    n = x.shape[0]
+    a, b = ga.shape[-1], gb.shape[-1]
+    f = pa.shape[-1]
+    opp = NZ // 2
+    bf, f32 = jnp.bfloat16, jnp.float32
+
+    def zc(k):
+        return lax.rem(z + (k + NZ), NZ)
+
+    def yc(k):
+        return lax.rem(y + k, NY)
+
+    def at(yy, zz):
+        return {"req": yy * NZ + zz}
+
+    nbr = (at(y, zc(1)), at(y, zc(-1)))
+    pending = []
+
+    def rcopy(src, dst, ssem, rsem, dev):
+        return pltpu.make_async_remote_copy(src_ref=src, dst_ref=dst, send_sem=ssem, recv_sem=rsem, device_id=dev, device_id_type=MESH)
+
+    def send(*args):
+        c = rcopy(*args)
+        c.start()
+        pending.append(c)
+
+    def took(dst, ssem, rsem, dev):
+        rcopy(dst, dst, ssem, rsem, dev).wait_recv()
+
+    own_gu = pltpu.make_async_copy(gu_h, raw.at[0], load_sem.at[0])
+    own_dn = pltpu.make_async_copy(dn_h, dn.at[0], load_sem.at[1])
+    own_gu.start()
+    own_dn.start()
+
+    barrier = pltpu.get_barrier_semaphore()
+    greet = [at(yc(k), z) for k in range(1, NY)] + [nbr[0], nbr[1]]
+    greet += [{"tp": lax.rem(tp + k, n_tp)} for k in range(1, n_tp)] + [{"rep": 1 - rep}]
+    for dev in greet:
+        pl.semaphore_signal(barrier, inc=1, device_id=dev, device_id_type=MESH)
+    pl.semaphore_wait(barrier, len(greet))
+
+    HALF = ((0, 1), (2, 3))
+    xa, xb = x.at[:, 0:a], x.at[:, a:a + b]
+    for k in range(1, NY):
+        send(xa, ga.at[z, y], a1_s.at[k], a1_r.at[y], at(yc(k), z))
+    for d in (0, 1):
+        send(xb, gb.at[z, y], b1_s.at[d, 1], b1_r.at[d, 1], nbr[d])
+    for d in (0, 1):
+        send(xa, ga.at[z, y], a2_s.at[d, 1, y], a2_r.at[d, 1, y], nbr[d])
+    for k in range(1, NY):
+        send(xb, gb.at[z, y], b2_s.at[0, k], b2_r.at[z, y], at(yc(k), z))
+    partner = {"rep": 1 - rep}
+    send(gu_h, raw.at[1], wx_s.at[0], wx_r.at[0], partner)
+    send(dn_h, dn.at[1], wx_s.at[1], wx_r.at[1], partner)
+    ga[z, y] = x[:, 0:a]
+    gb[z, y] = x[:, a:a + b]
+
+    for k in range(1, NY):
+        yb = yc(k)
+        took(ga.at[z, yb], a1_s.at[k], a1_r.at[yb], at(yb, z))
+        for d in (0, 1):
+            send(ga.at[z, yb], ga.at[z, yb], a2_s.at[d, 1, yb], a2_r.at[d, 1, yb], nbr[d])
+
+    part = wide.shape[0]
+
+    def split(j):
+        def step(i, carry):
+            start = pl.multiple_of(i * part, part)
+            wide[...] = raw[j, pl.ds(start, part), :].astype(f32)
+            rows = pl.ds(pl.multiple_of(i * (part // 2), part // 2), part // 2)
+            gu[j, rows, 0:128] = wide[pl.ds(0, part // 2, stride=2), :].astype(bf)
+            gu[j, rows, 128:256] = wide[pl.ds(1, part // 2, stride=2), :].astype(bf)
+            return carry
+        lax.fori_loop(0, raw.shape[1] // part, step, 0)
+
+    own_gu.wait()
+    split(0)
+
+    number = (rep * n_req + req, (1 - rep) * n_req + req)
+
+    def compute(zs):
+        m = len(zs) * NY * n
+        rows_a = jnp.concatenate([ga[zz].reshape(NY * n, a) for zz in zs], axis=0)
+        rows_b = jnp.concatenate([gb[zz].reshape(NY * n, b) for zz in zs], axis=0)
+        table = rows_a[:, 0:GATE_LANES].astype(f32)
+        expert = lax.rem(lax.broadcasted_iota(jnp.int32, table.shape, 1), GATE_LANES // 2)
+        acts = []
+        for j in (0, 1):
+            weight = jnp.sum(jnp.where(expert == number[j], table, 0.0), axis=1, keepdims=True)
+            cut = a - GATE_LANES
+            pr = jnp.dot(rows_a[:, GATE_LANES:], gu[j, 0:cut, :], preferred_element_type=f32)
+            pr = pr + jnp.dot(rows_b, gu[j, cut:cut + b, :], preferred_element_type=f32)
+            g, u = pr[:, 0:128], pr[:, 128:256]
+            acts.append((g / (1.0 + jnp.exp(-g)) * u * weight).astype(bf))
+        o = jnp.dot(acts[0], dn[0], preferred_element_type=f32) + jnp.dot(acts[1], dn[1], preferred_element_type=f32)
+        for i, zz in enumerate(zs):
+            block = o[i * NY * n:(i + 1) * NY * n]
+            pa[zz] = block[:, 0:f].reshape(NY, n, f)
+            pb[zz] = block[:, f:2 * f].reshape(NY, n, f)
+            by_s[zz] = block[:, f:2 * f].astype(bf).reshape(NY, n, f)
+            for k in range(1, NY):
+                send(by_s.at[zz, yc(k)], by_r.at[zz, y], rby_s.at[zz, k], rby_r.at[zz, y], at(yc(k), z))
+
+    def took_b2(zz):
+        for k in range(1, NY):
+            took(gb.at[zz, yc(k)], b2_s.at[0, k], b2_r.at[zz, yc(k)], at(yc(k), z))
+
+    h = b // 2
+    for s in range(1, opp + 1):
+        for d in (0, 1):
+            zz = zc(-s) if d == 0 else zc(s)
+            if s < opp:
+                took(gb.at[zz, y], b1_s.at[d, s], b1_r.at[d, s], nbr[d])
+                block = gb.at[zz, y] if s + 1 < opp else gb.at[zz, y, :, d * h:(d + 1) * h]
+                send(block, block, b1_s.at[d, s + 1], b1_r.at[d, s + 1], nbr[d])
+                for k in range(1, NY):
+                    send(gb.at[zz, y], gb.at[zz, y], b2_s.at[2 * s - 1 + d, k], b2_r.at[zz, y], at(yc(k), z))
+            else:
+                block = gb.at[zz, y, :, d * h:(d + 1) * h]
+                took(block, b1_s.at[d, s], b1_r.at[d, s], nbr[d])
+                if d == 1:
+                    for k in range(1, NY):
+                        send(gb.at[zz, y], gb.at[zz, y], b2_s.at[2 * s - 1, k], b2_r.at[zz, y], at(yc(k), z))
+        for d in (0, 1):
+            zz = zc(-s) if d == 0 else zc(s)
+            for yb in range(NY) if s < opp else HALF[d]:
+                took(ga.at[zz, yb], a2_s.at[d, s, yb], a2_r.at[d, s, yb], nbr[d])
+                if s + 1 < opp or (s + 1 == opp and yb in HALF[d]):
+                    send(ga.at[zz, yb], ga.at[zz, yb], a2_s.at[d, s + 1, yb], a2_r.at[d, s + 1, yb], nbr[d])
+        if s == 1:
+            own_dn.wait()
+            took(raw.at[1], wx_s.at[0], wx_r.at[0], partner)
+            took(dn.at[1], wx_s.at[1], wx_r.at[1], partner)
+            split(1)
+            took_b2(z)
+            compute([z])
+        else:
+            near = [zc(-(s - 1)), zc(s - 1)]
+            for zz in near:
+                took_b2(zz)
+            compute(near)
+    far = zc(opp)
+    took_b2(far)
+    compute([far])
+
+    def a_send(d, k, yb, value):
+        sa[d, k, yb] = value.astype(bf)
+        send(sa.at[d, k, yb], ra.at[d, k, yb], rsa_s.at[d, k, yb], rsa_r.at[d, k, yb], nbr[d])
+
+    def a_step(k):
+        for d in (0, 1):
+            zz = zc(k) if d == 0 else zc(-k)
+            for yb in range(NY) if k < opp else HALF[d]:
+                value = pa[zz, yb]
+                if k < opp - 1 or (k == opp - 1 and yb in HALF[d]):
+                    took(ra.at[d, k + 1, yb], rsa_s.at[d, k + 1, yb], rsa_r.at[d, k + 1, yb], nbr[d])
+                    value = value + ra[d, k + 1, yb].astype(f32)
+                a_send(d, k, yb, value)
+
+    def b_own(zz):
+        value = pb[zz, y]
+        for k in range(1, NY):
+            took(by_r.at[zz, yc(k)], rby_s.at[zz, k], rby_r.at[zz, yc(k)], at(yc(k), z))
+            value = value + by_r[zz, yc(k)].astype(f32)
+        return value
+
+    e = f // 2
+
+    def b_step(k):
+        if k == opp:
+            value = b_own(zc(k)).astype(bf)
+            for d in (0, 1):
+                sb[d, k, :, d * e:(d + 1) * e] = value[:, d * e:(d + 1) * e]
+                send(sb.at[d, k, :, d * e:(d + 1) * e], rb.at[d, k, :, d * e:(d + 1) * e], rsb_s.at[d, k], rsb_r.at[d, k], nbr[d])
+            return
+        for d in (0, 1):
+            value = b_own(zc(k) if d == 0 else zc(-k))
+            if k == opp - 1:
+                part = rb.at[d, k + 1, :, d * e:(d + 1) * e]
+                took(part, rsb_s.at[d, k + 1], rsb_r.at[d, k + 1], nbr[d])
+                added = value[:, d * e:(d + 1) * e] + rb[d, k + 1, :, d * e:(d + 1) * e].astype(f32)
+                value = jnp.concatenate([added, value[:, e:]] if d == 0 else [value[:, :e], added], axis=1)
+            else:
+                took(rb.at[d, k + 1], rsb_s.at[d, k + 1], rsb_r.at[d, k + 1], nbr[d])
+                value = value + rb[d, k + 1].astype(f32)
+            sb[d, k] = value.astype(bf)
+            send(sb.at[d, k], rb.at[d, k], rsb_s.at[d, k], rsb_r.at[d, k], nbr[d])
+
+    a_step(4)
+    a_step(3)
+    b_step(4)
+    a_step(2)
+    b_step(3)
+    a_step(1)
+    b_step(2)
+    total_a = None
+    for k in (1, 2, 3, 0):
+        yb = yc(k)
+        value = pa[z, yb]
+        for d in (0, 1):
+            took(ra.at[d, 1, yb], rsa_s.at[d, 1, yb], rsa_r.at[d, 1, yb], nbr[d])
+            value = value + ra[d, 1, yb].astype(f32)
+        if k:
+            ys[yb] = value.astype(bf)
+            send(ys.at[yb], yr.at[y], ry_s.at[k], ry_r.at[y], at(yb, z))
+        else:
+            total_a = value
+    b_step(1)
+    total_b = b_own(z)
+    for d in (0, 1):
+        took(rb.at[d, 1], rsb_s.at[d, 1], rsb_r.at[d, 1], nbr[d])
+        total_b = total_b + rb[d, 1].astype(f32)
+    for k in range(1, NY):
+        yb = yc(k)
+        took(yr.at[yb], ry_s.at[k], ry_r.at[yb], at(yb, z))
+        total_a = total_a + yr[yb].astype(f32)
+
+    width = out.shape[1]
+    total = jnp.concatenate([total_a, total_b], axis=1)
+    for t in range(n_tp):
+        quarter = total[:, t * width:(t + 1) * width]
+        xf[t] = quarter
+        xs[t] = quarter.astype(bf)
+    for k in range(1, n_tp):
+        t = lax.rem(tp + k, n_tp)
+        send(xs.at[t], xr.at[tp], rx_s.at[k], rx_r.at[tp], {"tp": t})
+    value = res[...] + xf[tp]
+    for k in range(1, n_tp):
+        t = lax.rem(tp + k, n_tp)
+        took(xr.at[t], rx_s.at[k], rx_r.at[t], {"tp": t})
+        value = value + xr[t].astype(f32)
+    out[...] = value.astype(bf)
+    for c in pending:
+        c.wait_send()
+
+
+def experts(n_tp, n_req, x, res, w_gateup, w_down):
+    n, wide = x.shape
+    width = res.shape[1]
+    model = w_down.shape[2]
+    a = GATE_LANES + model // 2
+    b = model // 2
+    f = model // 2
+    gu = w_gateup.reshape(2 * model, w_gateup.shape[3])
+    dn = w_down[0]
+    vmem, hbm = pl.BlockSpec(memory_space=pltpu.VMEM), pl.BlockSpec(memory_space=pl.ANY)
+    bf, f32 = jnp.bfloat16, jnp.float32
+    dma = pltpu.SemaphoreType.DMA
+    v = pltpu.VMEM
+    k5 = NZ // 2 + 1
+    return pl.pallas_call(
+        functools.partial(experts_kernel, n_tp, n_req),
+        name="experts",
+        out_shape=jax.ShapeDtypeStruct((n, width), bf),
+        in_specs=[vmem, vmem, hbm, hbm],
+        out_specs=vmem,
+        scratch_shapes=[
+            v((NZ, NY, n, a), bf), v((NZ, NY, n, b), bf), v((NZ, NY, n, f), f32), v((NZ, NY, n, f), f32),
+            v((2,) + gu.shape, bf), v((512, 128), f32), v((2, model, 256), bf), v((2,) + dn.shape, bf),
+            v((NZ, NY, n, f), bf), v((NZ, NY, n, f), bf),
+            v((2, k5, NY, n, f), bf), v((2, k5, NY, n, f), bf), v((2, k5, n, f), bf), v((2, k5, n, f), bf),
+            v((NY, n, f), bf), v((NY, n, f), bf), v((n_tp, n, width), bf), v((n_tp, n, width), bf), v((n_tp, n, width), f32),
+            dma((2,)), dma((2,)), dma((2,)), dma((NY,)), dma((NY,)), dma((2, k5, NY)), dma((2, k5, NY)), dma((2, k5)), dma((2, k5)),
+            dma((NZ, NY)), dma((NZ, NY)),
+            dma((NZ, NY)), dma((NZ, NY)), dma((2, k5, NY)), dma((2, k5, NY)), dma((2, k5)), dma((2, k5)), dma((NY,)), dma((NY,)),
+            dma((n_tp,)), dma((n_tp,)),
+        ],
+        compiler_params=pltpu.CompilerParams(collective_id=1, has_side_effects=True, vmem_limit_bytes=67_000_000),
+        cost_estimate=pl.CostEstimate(flops=1_300_000_000, bytes_accessed=4_000_000, transcendentals=200_000),
+    )(x, res, gu, dn)
 
 
 def shards(
@@ -252,55 +538,11 @@
     expert_ids,
     expert_gates,
 ):
-    row_count = hidden.shape[0]
-    x, own_residual = attention(lax.axis_size('tp'), lengths, migrate, hidden, kv_cache, attn_gain, moe_gain, w_query, key_value_weight, output_weight, expert_ids, expert_gates)
-    expert_in = x[:, GATE_LANES:]
-    expert_count = lax.axis_size("rep") * lax.axis_size("req")
-    top_count = expert_ids.shape[1]
-    capacity = min(row_count, max(3, 3 * row_count * top_count // expert_count))
-    flat_ids = expert_ids.reshape(-1)
-    matches = (flat_ids[:, None] == jnp.arange(expert_count, dtype=jnp.int32)[None, :]).astype(
-        jnp.int32
-    )
-    slot_rank = jnp.sum((jnp.cumsum(matches, axis=0) - matches) * matches, axis=1)
-    slot_target = flat_ids * capacity + slot_rank
-    slot_table = (
-        slot_target[:, None] == jnp.arange(expert_count * capacity, dtype=jnp.int32)[None, :]
-    ).astype(jnp.float32)
-    route_table = slot_table.reshape(row_count, top_count, -1).sum(axis=1)
-    gate_table = (
-        (slot_table * expert_gates.reshape(-1, 1)).reshape(row_count, top_count, -1).sum(axis=1)
-    )
-    outbound = jnp.einsum(
-        "rs,rd->sd", route_table.astype(jnp.bfloat16), expert_in, preferred_element_type=jnp.float32
-    ).astype(jnp.bfloat16)
-    outbound = outbound.reshape(expert_count, capacity, -1)
-    gate_up = w_gateup[0].reshape(w_gateup.shape[1], -1)
-    down_rows = w_down[0]
-    arrived_rows = lax.all_to_all(outbound, ("rep", "req"), split_axis=0, concat_axis=0, tiled=True)
-    model_width = arrived_rows.shape[2]
-    flattened = arrived_rows.reshape(-1, model_width)
-    projected = jnp.dot(flattened, gate_up, preferred_element_type=jnp.float32)
-    split_at = projected.shape[1] // 2
-    activation = (jax.nn.silu(projected[:, :split_at]) * projected[:, split_at:]).astype(
-        jnp.bfloat16
-    )
-    expert_part = jnp.dot(activation, down_rows, preferred_element_type=jnp.float32)
-    expert_part = expert_part.reshape(arrived_rows.shape[0], arrived_rows.shape[1], model_width)
-    returned = lax.all_to_all(
-        expert_part.astype(jnp.bfloat16), ("rep", "req"), split_axis=0, concat_axis=0, tiled=True
-    ).astype(expert_part.dtype)
-    returned_rows = returned.reshape(expert_count * capacity, -1)
-    combined = jnp.dot(
-        gate_table,
-        returned_rows,
-        precision=lax.Precision.HIGHEST,
-        preferred_element_type=jnp.float32,
-    )
-    expert_mix = lax.psum_scatter(
-        combined.astype(jnp.bfloat16), "tp", scatter_dimension=1, tiled=True
-    ).astype(jnp.float32)
-    return (own_residual + expert_mix).astype(jnp.bfloat16)
+    n_tp, n_req = lax.axis_size("tp"), lax.axis_size("req")
+    x, res = attention(
+        n_tp, lengths, migrate, hidden, kv_cache, attn_gain, moe_gain, w_query, key_value_weight, output_weight,
+        expert_ids, expert_gates)
+    return experts(n_tp, n_req, x, res, w_gateup, w_down)
 
 
 def solution(mesh):

time: 174 us -> 88.7 us (0.51)
  blocking collectives: 97.8 us -> 0 us
  Pallas kernels: 23.1 us -> 80.7 us
  waiting for transfers between devices: 18.7 us -> 0 us
  between operations: 14.2 us -> 0.67 us
  local copies, waits for them, and re-layouts: 16 us -> 6.47 us
  matrix products: 1.97 us -> 0 us
    all_to_all x2 -> x0, blocking collectives: 97.8 us -> none  [the longest x1 51.9 us: shards(): lax.all_to_all(outbound, ('rep', 'req'), split_axis=0, concat_axis=0, til...]
    pallas_call x0 -> x1, Pallas kernels: none -> 57.2 us  [experts(): pl.pallas_call(functools.partial(experts_kernel, n_tp, n_req), name='expe...]
    unnamed x2 -> x0, waiting for transfers between devices: 18.7 us -> none
    unnamed x20 -> x1, local copies, waits for them, and re-layouts: 9.12 us -> 1.31 us
    reshape x3 -> x0, local copies, waits for them, and re-layouts: 3.21 us -> none  [the longest x1 2.36 us: shards(): flattened = arrived_rows.reshape(-1, model_width)]
    dot_general x4 -> x0, matrix products: 1.97 us -> none  [the longest x1 0.56 us: shards(): jnp.dot(gate_table, returned_rows, precision=lax.Precision.HIGHEST, prefe...]
  transfers between devices with their start and end apart: 1 -> 0, of which waited for: 1 -> 0; matrix products, arithmetic and copies ran while one was open for 0% -> 0% of each run, Pallas kernels for 0% -> 0%
where the time goes in v2:
time: 88.7 us; the launch traced here: 87.8 us
  Pallas kernels  80.7 us (91%)
  local copies, waits for them, and re-layouts  6.47 us (7%)
    pallas_call x1, Pallas kernels, experts(): pl.pallas_call(functools.partial(experts_kernel, n_tp, n_req), name='expe...  57.2 us
    pallas_call x1, Pallas kernels, attention(): pl.pallas_call(functools.partial(attention_kernel, n_tp), name='attention...  23.5 us

profile of v2, /device:TPU:8, one launch (start us, length us, event | category | flops | bytes accessed | tf_op | source)
XLA Modules:
  0.0 87.8 jit_solution(9072905099396754986)
XLA Ops:
  0.7 1.3 %pad.8.ids = s32[8,128]{1,0:T(8,128)} pad(s32[8,16]{1,0:T(8,128)} %bitcast.6, s32[]{:T(128)} %constant.4.clone.1), padding=0_0x0_112 | pad | bytes 4612 | tf_op jit(solution)/shard_map/jit(_pad)/pad | solution.py:214
  1.9 1.3 %pad.9.gates = f32[8,128]{1,0:T(8,128)} pad(f32[8,16]{1,0:T(8,128)} %bitcast.7, f32[]{:T(128)} %constant.5.clone.1), padding=0_0x0_112 | pad | bytes 4612 | tf_op jit(solution)/shard_map/jit(_pad)/pad | solution.py:215
  3.2 1.3 %reshape.13.ag = f32[1,1536]{1,0:T(1,128)} reshape(f32[1536]{0:T(1024)} %param.18) | data formatting | bytes 12288 | tf_op jit(solution)/shard_map/reshape | solution.py:237
  4.5 1.3 %reshape.14.mg = f32[1,1536]{1,0:T(1,128)} reshape(f32[1536]{0:T(1024)} %param.19) | data formatting | bytes 12288 | tf_op jit(solution)/shard_map/reshape | solution.py:237
  5.8 23.5 %attention.1 = (bf16[16,1664]{1,0:T(8,128)(2,1)}, f32[16,384]{1,0:T(8,128)}) custom-call(s32[2,16]{1,0:T(2,128)} %len_s.1, s32[1]{0:T(128)S(6)} %copy.16.mig_s, bf16[16,384]{1,0:T(8,128)(2,1)} %hid.1, bf16[16,2048,128]{2,1,0:T(8,128)(2,1)} %bitcast.5, f32[1,1536]{1,0:T(1,128)} %reshape.13.ag, f32[1,1536]{1,0:T(1,128)} %reshape.14.mg, ...), custom_call_target="tpu_custom_call" | custom-call | flops 200000000 | bytes 12000000 | tf_op jit(solution)/shard_map/attention/pallas_call | solution.py:219
  29.3 57.2 %experts.1 = bf16[16,384]{1,0:T(8,128)(2,1)} custom-call(bf16[16,1664]{1,0:T(8,128)(2,1)} %get-tuple-element.7.x, f32[16,384]{1,0:T(8,128)} %get-tuple-element.8.res, bf16[3072,128]{1,0:T(8,128)(2,1)} %bitcast.8, bf16[128,1536]{1,0:T(8,128)(2,1)} %bitcast.9), custom_call_target="tpu_custom_call" | custom-call | flops 1300000000 | bytes 4000000 | tf_op jit(solution)/shard_map/experts/pallas_call | solution.py:504
  86.5 1.3 %copy.17 = bf16[16,384]{1,0:T(8,128)(2,1)} copy(bf16[16,384]{1,0:T(8,128)(2,1)} %experts.1) | data formatting | bytes 24576

commit v3 on v1

v3 whole, which is shorter than its diff:
```python
import functools
import jax
import jax.numpy as jnp
import numpy as np
from jax import lax
from jax.experimental import pallas as pl
from jax.experimental.pallas import tpu as pltpu
from jax.sharding import PartitionSpec as P

MESH = pl.DeviceIdType.MESH
HEAD_SIZE = 64
EPSILON = 1e-06
ROPE_BASE = 10000.0
MASKED = -1e30
GATE_LANES = 128
NY, NZ = 4, 8
VMEM_LIMIT = 58 * 2**20


def rows_of(scalars, n):
    row = lax.broadcasted_iota(jnp.int32, (n, 128), 0)
    out = jnp.zeros((n, 128), jnp.int32)
    for r in range(n):
        out = jnp.where(row == r, scalars(r), out)
    return out


def attend(q, kvn, kv, bias, limit):
    scale = HEAD_SIZE ** (-0.5)
    s = lax.dot_general(q.astype(jnp.bfloat16), kv, (((1,), (1,)), ((), ())), preferred_element_type=jnp.float32)
    lane = lax.broadcasted_iota(jnp.int32, s.shape, 1)
    s = jnp.where(lane < limit, s * scale + bias, MASKED)
    own = jnp.sum(q * kvn, axis=1, keepdims=True) * scale
    peak = jnp.maximum(jnp.max(s, axis=1, keepdims=True), own)
    p = jnp.exp(s - peak)
    p_own = jnp.exp(own - peak)
    inv = 1.0 / (jnp.sum(p, axis=1, keepdims=True) + p_own)
    w = (p * inv).astype(jnp.bfloat16)
    w_own = (p_own * inv).astype(jnp.bfloat16).astype(jnp.float32)
    return jnp.dot(w, kv, preferred_element_type=jnp.float32) + w_own * kvn


def layer_kernel(
    n_tp, n_req,
    len_h, mig_s, hid_h, kv_h, ag_h, mg_h, freq_h, wq_h, wkv_h, wo_h, ids_h, gates_h, gu_h, dn_h,
    out,
    len_s, hid, ag, mg, freq, ids, gates,
    kv_v, wq_v, wkv_v, wo_v, tok, kv_send, kv_recv, part_send, part_recv, q_s, kvn_s, ctx_s, bias_s,
    ga, gb, pa, pb, raw, wide, gu, dn,
    by_s, by_r, sa, ra, sb, rb, ys, yr, xs, xr, xf,
    load_sem, kv_sem, tok_send_sem, tok_recv_sem, kv_send_sem, kv_recv_sem, part_send_sem, part_recv_sem,
    wx_s, wx_r, a1_s, a1_r, a2_s, a2_r, b1_s, b1_r, b2_s, b2_r,
    rby_s, rby_r, rsa_s, rsa_r, rsb_s, rsb_r, ry_s, ry_r, rx_s, rx_r,
):
    rep, req, tp = lax.axis_index("rep"), lax.axis_index("req"), lax.axis_index("tp")
    y, z = req // NZ, lax.rem(req, NZ)
    n, width = hid.shape
    heads = wq_v.shape[1] // HEAD_SIZE
    kvh = wkv_v.shape[1] // (2 * HEAD_SIZE)
    group = heads // kvh
    n_lanes = kv_v.shape[1]
    a, b, f = ga.shape[-1], gb.shape[-1], pa.shape[-1]
    opp = NZ // 2
    bf, f32 = jnp.bfloat16, jnp.float32

    def zc(k):
        return lax.rem(z + (k + NZ), NZ)

    def yc(k):
        return lax.rem(y + k, NY)

    def tc(k):
        return lax.rem(tp + k, n_tp)

    def at(yy, zz):
        return {"req": yy * NZ + zz}

    nbr = (at(y, zc(1)), at(y, zc(-1)))
    partner = {"rep": 1 - rep}
    pending = []

    def rcopy(src, dst, ssem, rsem, dev):
        return pltpu.make_async_remote_copy(src_ref=src, dst_ref=dst, send_sem=ssem, recv_sem=rsem, device_id=dev, device_id_type=MESH)

    def send(*args):
        c = rcopy(*args)
        c.start()
        pending.append(c)

    def took(dst, ssem, rsem, dev):
        rcopy(dst, dst, ssem, rsem, dev).wait_recv()

    loads = []

    def load(src, dst):
        c = pltpu.make_async_copy(src, dst, load_sem.at[len(loads)])
        c.start()
        loads.append(c)
        return c

    small = [load(*p) for p in ((hid_h, hid), (len_h, len_s), (ids_h, ids), (gates_h, gates), (freq_h, freq), (ag_h, ag), (mg_h, mg))]
    proj = [load(wq_h, wq_v), load(wkv_h, wkv_v)]
    kv_loads = [pltpu.make_async_copy(kv_h.at[r], kv_v.at[r], kv_sem.at[r]) for r in range(n)]
    for c in kv_loads:
        c.start()
    load_o = load(wo_h, wo_v)
    own_gu = load(gu_h, raw.at[0])
    own_dn = load(dn_h, dn.at[0])

    barrier = pltpu.get_barrier_semaphore()
    peers = [(0, tc(k)) for k in range(1, n_tp)] + [(1, tc(k)) for k in range(n_tp)]
    far_rep = lambda side: rep if side == 0 else 1 - rep
    greet = [{"rep": far_rep(side), "tp": t} for side, t in peers]
    greet += [at(yc(k), z) for k in range(1, NY)] + [nbr[0], nbr[1]]
    for dev in greet:
        pl.semaphore_signal(barrier, inc=1, device_id=dev, device_id_type=MESH)
    pl.semaphore_wait(barrier, len(greet))

    for c in small:
        c.wait()
    for i, (side, t) in enumerate(peers):
        send(hid, tok.at[side, tp], tok_send_sem.at[i], tok_recv_sem.at[side, tp], {"rep": far_rep(side), "tp": t})
    tok[0, tp] = hid[...]
    send(gu_h, raw.at[1], wx_s.at[0], wx_r.at[0], partner)
    send(dn_h, dn.at[1], wx_s.at[1], wx_r.at[1], partner)

    slot = mig_s[0]
    row = lax.broadcasted_iota(jnp.int32, (n, 128), 0)
    lane = lax.broadcasted_iota(jnp.int32, (n, 128), 1)
    moved = row == slot
    own_span = rows_of(lambda r: jnp.where(rep == 0, len_s[0, r], len_s[1, r]), n)
    other_span = rows_of(lambda r: jnp.where(rep == 0, len_s[1, r], len_s[0, r]), n)
    span = jnp.where(moved, other_span, own_span).astype(f32)
    angle = span * freq[...]
    cosine, sine = jnp.cos(angle), jnp.sin(angle)
    first = lax.rem(lane, HEAD_SIZE) < HEAD_SIZE // 2
    half = HEAD_SIZE // 2

    def rotate(v):
        turned = jnp.where(first, -pltpu.roll(v, 128 - half, 1), pltpu.roll(v, half, 1))
        return v * cosine + turned * sine

    head = lax.broadcasted_iota(jnp.int32, (8, n_lanes), 0)
    pos = lax.broadcasted_iota(jnp.int32, (8, n_lanes), 1)
    bias_s[...] = jnp.where(lax.rem(pos, kvh) == head // group, 0.0, MASKED)

    eye = lax.broadcasted_iota(jnp.int32, (n, n), 0) == lax.broadcasted_iota(jnp.int32, (n, n), 1)
    expert = lax.rem(lane, GATE_LANES // 2)
    dense = jnp.zeros((n, 128), f32)
    for k in range(ids.shape[0]):
        idc = jnp.sum(jnp.where(eye, ids[k:k + 1, :], 0), axis=1, keepdims=True)
        gc = jnp.sum(jnp.where(eye, gates[k:k + 1, :], 0.0), axis=1, keepdims=True)
        dense = dense + jnp.where(expert == idc, gc, 0.0)
    high = dense.astype(bf).astype(f32)
    ga[z, y, :, 0:GATE_LANES] = jnp.where(lane < GATE_LANES // 2, high, dense - high).astype(bf)

    part = wide.shape[0]

    def split(j):
        def step(i, carry):
            start = pl.multiple_of(i * part, part)
            wide[...] = raw[j, pl.ds(start, part), :].astype(f32)
            rows = pl.ds(pl.multiple_of(i * (part // 2), part // 2), part // 2)
            gu[j, rows, 0:128] = wide[pl.ds(0, part // 2, stride=2), :].astype(bf)
            gu[j, rows, 128:256] = wide[pl.ds(1, part // 2, stride=2), :].astype(bf)
            return carry
        lax.fori_loop(0, raw.shape[1] // part, step, 0)

    for side, t in peers:
        took(tok.at[side, t], tok_send_sem.at[0], tok_recv_sem.at[side, t], {"tp": t})

    moved_w = lax.broadcasted_iota(jnp.int32, (n, width), 0) == slot
    tokens = jnp.concatenate(
        [jnp.where(moved_w, tok[1, t].astype(f32), tok[0, t].astype(f32)) for t in range(n_tp)], axis=1)
    mean = jnp.mean(tokens * tokens, axis=1, keepdims=True)
    gain = jnp.concatenate([ag[i:i + 1, :] for i in range(ag.shape[0])], axis=1)
    normed = (tokens * lax.rsqrt(mean + EPSILON) * gain).astype(bf)
    for c in proj:
        c.wait()
    queries = jnp.dot(normed, wq_v[...], preferred_element_type=f32)
    keyval = jnp.dot(normed, wkv_v[...], preferred_element_type=f32)
    q_s[...] = jnp.zeros_like(q_s)
    kvn_s[...] = jnp.zeros_like(kvn_s)
    low_lanes = lane < HEAD_SIZE
    for i in range(heads // 2):
        turned = rotate(queries[:, i * 128:(i + 1) * 128]).astype(bf).astype(f32)
        q_s[:, 2 * i, :] = jnp.where(low_lanes, turned, 0.0)
        q_s[:, 2 * i + 1, :] = jnp.where(low_lanes, pltpu.roll(turned, HEAD_SIZE, 1), 0.0)
    for g in range(kvh):
        both = keyval[:, g * 128:(g + 1) * 128]
        both = jnp.where(low_lanes, rotate(both), both).astype(bf).astype(f32)
        for h in range(g * group, (g + 1) * group):
            kvn_s[:, h, :] = both

    for c in kv_loads:
        c.wait()
    kv_send[...] = kv_v[slot]
    kv_copy = rcopy(kv_send, kv_recv, kv_send_sem, kv_recv_sem, partner)
    kv_copy.start()

    def one(r):
        limit = kvh * jnp.where(rep == 0, len_s[0, r], len_s[1, r])
        ctx_s[r] = attend(q_s[r], kvn_s[r], kv_v[r], bias_s[...], limit)

    UNROLL = 4

    def step(i, carry):
        for j in range(UNROLL):
            one(i * UNROLL + j)
        return carry

    lax.fori_loop(0, n // UNROLL, step, 0)
    kv_copy.wait()
    limit = kvh * jnp.where(rep == 0, len_s[1, slot], len_s[0, slot])
    arrived = attend(q_s[slot], kvn_s[slot], kv_recv[...], bias_s[...], limit)

    blocks = []
    for i in range(heads // 2):
        even = jnp.where(moved, arrived[2 * i:2 * i + 1], ctx_s[:, 2 * i, :])
        odd = jnp.where(moved, arrived[2 * i + 1:2 * i + 2], ctx_s[:, 2 * i + 1, :])
        blocks.append(jnp.where(low_lanes, pltpu.roll(even, HEAD_SIZE, 1), odd))
    context = jnp.concatenate(blocks, axis=1).astype(bf)
    load_o.wait()
    partial = jnp.dot(context, wo_v[...], preferred_element_type=f32)
    part_send[...] = partial.astype(bf)
    for k in (1, 3, 2):
        send(part_send, part_recv.at[tp], part_send_sem.at[k], part_recv_sem.at[tp], {"tp": tc(k)})
    own_gu.wait()
    own_dn.wait()
    split(0)
    took(raw.at[1], wx_s.at[0], wx_r.at[0], partner)
    took(dn.at[1], wx_s.at[1], wx_r.at[1], partner)
    split(1)
    total = tokens + partial
    for k in (1, 3, 2):
        t = tc(k)
        took(part_recv.at[t], part_send_sem.at[k], part_recv_sem.at[t], {"tp": t})
        total = total + part_recv[t].astype(f32)
    mean = jnp.mean(total * total, axis=1, keepdims=True)
    gain = jnp.concatenate([mg[i:i + 1, :] for i in range(mg.shape[0])], axis=1)
    x = (total * lax.rsqrt(mean + EPSILON) * gain).astype(bf)
    cut = a - GATE_LANES
    ga[z, y, :, GATE_LANES:] = x[:, 0:cut]
    gb[z, y] = x[:, cut:]

    ORDER = (0, 1, 3, 2)
    REL = ((0, 1), (3, 2))
    AWAY = (1, 3, 2)
    for d in (0, 1):
        send(ga.at[z, y], ga.at[z, y], a2_s.at[d, 1, 0], a2_r.at[d, 1, 0], nbr[d])
    for k in AWAY:
        send(ga.at[z, y], ga.at[z, y], a1_s.at[k], a1_r.at[y], at(yc(k), z))
    for d in (0, 1):
        send(gb.at[z, y], gb.at[z, y], b1_s.at[d, 1], b1_r.at[d, 1], nbr[d])
    for k in AWAY:
        send(gb.at[z, y], gb.at[z, y], b2_s.at[0, k], b2_r.at[z, y], at(yc(k), z))
    own = jnp.zeros((n, width), f32)
    for t in range(n_tp):
        own = jnp.where(tp == t, total[:, t * width:(t + 1) * width], own)
    xf[n_tp] = own
    for k in AWAY:
        yb = yc(k)
        took(ga.at[z, yb], a1_s.at[k], a1_r.at[yb], at(yb, z))
        for d in (0, 1):
            send(ga.at[z, yb], ga.at[z, yb], a2_s.at[d, 1, k], a2_r.at[d, 1, k], nbr[d])

    number = (rep * n_req + req, (1 - rep) * n_req + req)

    def compute(zs):
        rows_a = jnp.concatenate([ga[zz].reshape(NY * n, a) for zz in zs], axis=0)
        rows_b = jnp.concatenate([gb[zz].reshape(NY * n, b) for zz in zs], axis=0)
        table = rows_a[:, 0:GATE_LANES].astype(f32)
        which = lax.rem(lax.broadcasted_iota(jnp.int32, table.shape, 1), GATE_LANES // 2)
        acts = []
        for j in (0, 1):
            weight = jnp.sum(jnp.where(which == number[j], table, 0.0), axis=1, keepdims=True)
            pr = jnp.dot(rows_a[:, GATE_LANES:], gu[j, 0:cut, :], preferred_element_type=f32)
            pr = pr + jnp.dot(rows_b, gu[j, cut:cut + b, :], preferred_element_type=f32)
            g, u = pr[:, 0:128], pr[:, 128:256]
            acts.append((g / (1.0 + jnp.exp(-g)) * u * weight).astype(bf))
        o = jnp.dot(acts[0], dn[0], preferred_element_type=f32) + jnp.dot(acts[1], dn[1], preferred_element_type=f32)
        for i, zz in enumerate(zs):
            block = o[i * NY * n:(i + 1) * NY * n]
            pa[zz] = block[:, 0:f].reshape(NY, n, f)
            pb[zz] = block[:, f:2 * f].reshape(NY, n, f)
            by_s[zz] = block[:, f:2 * f].astype(bf).reshape(NY, n, f)
            for k in AWAY:
                send(by_s.at[zz, yc(k)], by_r.at[zz, y], rby_s.at[zz, k], rby_r.at[zz, y], at(yc(k), z))

    def chunk(s):
        zs = [zc(s)] if s in (0, opp) else [zc(-s), zc(s)]
        for zz in zs:
            for k in AWAY:
                took(gb.at[zz, yc(k)], b2_s.at[0, k], b2_r.at[zz, yc(k)], at(yc(k), z))
        compute(zs)

    def a_send(d, k, i, value):
        sa[d, k, i] = value.astype(bf)
        send(sa.at[d, k, i], ra.at[d, k, i], rsa_s.at[d, k, i], rsa_r.at[d, k, i], nbr[d])

    def a_took(d, k, i):
        took(ra.at[d, k, i], rsa_s.at[d, k, i], rsa_r.at[d, k, i], nbr[d])
        return ra[d, k, i].astype(f32)

    h = b // 2
    for s in range(1, opp + 1):
        for d in (0, 1):
            zz = zc(-s) if d == 0 else zc(s)
            if s < opp:
                took(gb.at[zz, y], b1_s.at[d, s], b1_r.at[d, s], nbr[d])
                block = gb.at[zz, y] if s + 1 < opp else gb.at[zz, y, :, d * h:(d + 1) * h]
                send(block, block, b1_s.at[d, s + 1], b1_r.at[d, s + 1], nbr[d])
            else:
                block = gb.at[zz, y, :, d * h:(d + 1) * h]
                took(block, b1_s.at[d, s], b1_r.at[d, s], nbr[d])
            if s < opp or d == 1:
                for k in AWAY:
                    send(gb.at[zz, y], gb.at[zz, y], b2_s.at[2 * s - 1 + d if s < opp else 2 * s - 1, k], b2_r.at[zz, y], at(yc(k), z))
        if s == opp:
            chunk(2)
            chunk(3)
            for d in (0, 1):
                for i in REL[1 - d]:
                    a_send(d, opp - 1, i, pa[zc(opp - 1) if d == 0 else zc(1 - opp), yc(i)])
        for i in ORDER:
            for d in (0, 1):
                if s == opp and i not in REL[d]:
                    continue
                zz = zc(-s) if d == 0 else zc(s)
                yb = yc(i)
                took(ga.at[zz, yb], a2_s.at[d, s, i], a2_r.at[d, s, i], nbr[d])
                if s + 1 < opp or (s + 1 == opp and i in REL[d]):
                    send(ga.at[zz, yb], ga.at[zz, yb], a2_s.at[d, s + 1, i], a2_r.at[d, s + 1, i], nbr[d])
        if s in (2, 3):
            chunk(s - 2)
    chunk(opp)

    def a_step(k):
        for i in ORDER:
            for d in (0, 1):
                if k >= opp - 1 and i not in REL[d]:
                    continue
                value = pa[zc(k) if d == 0 else zc(-k), yc(i)]
                if k < opp:
                    value = value + a_took(d, k + 1, i)
                a_send(d, k, i, value)

    def b_own(zz):
        value = pb[zz, y]
        for k in AWAY:
            took(by_r.at[zz, yc(k)], rby_s.at[zz, k], rby_r.at[zz, yc(k)], at(yc(k), z))
            value = value + by_r[zz, yc(k)].astype(f32)
        return value

    e = f // 2

    def b_step(k):
        if k == opp:
            value = b_own(zc(k)).astype(bf)
            for d in (0, 1):
                lanes = slice(d * e, (d + 1) * e)
                sb[d, k, :, lanes] = value[:, lanes]
                send(sb.at[d, k, :, lanes], rb.at[d, k, :, lanes], rsb_s.at[d, k], rsb_r.at[d, k], nbr[d])
            return
        for d in (0, 1):
            value = b_own(zc(k) if d == 0 else zc(-k))
            if k == opp - 1:
                lanes = slice(d * e, (d + 1) * e)
                took(rb.at[d, k + 1, :, lanes], rsb_s.at[d, k + 1], rsb_r.at[d, k + 1], nbr[d])
                added = value[:, lanes] + rb[d, k + 1, :, lanes].astype(f32)
                value = jnp.concatenate([added, value[:, e:]] if d == 0 else [value[:, :e], added], axis=1)
            else:
                took(rb.at[d, k + 1], rsb_s.at[d, k + 1], rsb_r.at[d, k + 1], nbr[d])
                value = value + rb[d, k + 1].astype(f32)
            sb[d, k] = value.astype(bf)
            send(sb.at[d, k], rb.at[d, k], rsb_s.at[d, k], rsb_r.at[d, k], nbr[d])

    a_step(4)
    a_step(3)
    b_step(4)
    a_step(2)
    b_step(3)
    a_step(1)
    b_step(2)
    for k in AWAY:
        yb = yc(k)
        ys[yb] = (pa[z, yb] + a_took(0, 1, k) + a_took(1, 1, k)).astype(bf)
        send(ys.at[yb], yr.at[y], ry_s.at[k], ry_r.at[y], at(yb, z))
    total_a = pa[z, y] + a_took(0, 1, 0) + a_took(1, 1, 0)
    b_step(1)
    total_b = b_own(z)
    for d in (0, 1):
        took(rb.at[d, 1], rsb_s.at[d, 1], rsb_r.at[d, 1], nbr[d])
        total_b = total_b + rb[d, 1].astype(f32)
    for k in AWAY:
        yb = yc(k)
        took(yr.at[yb], ry_s.at[k], ry_r.at[yb], at(yb, z))
        total_a = total_a + yr[yb].astype(f32)

    total = jnp.concatenate([total_a, total_b], axis=1)
    for t in range(n_tp):
        quarter = total[:, t * width:(t + 1) * width]
        xf[t] = quarter
        xs[t] = quarter.astype(bf)
    for k in AWAY:
        t = tc(k)
        send(xs.at[t], xr.at[tp], rx_s.at[k], rx_r.at[tp], {"tp": t})
    value = xf[n_tp] + xf[tp]
    for k in AWAY:
        t = tc(k)
        took(xr.at[t], rx_s.at[k], rx_r.at[t], {"tp": t})
        value = value + xr[t].astype(f32)
    out[...] = value.astype(bf)
    for c in pending:
        c.wait_send()


def layer(
    hidden, lengths, migrate, kv_cache, attn_gain, moe_gain, w_query, key_value_weight, output_weight,
    w_gateup, w_down, expert_ids, expert_gates,
):
    n_tp, n_req = lax.axis_size("tp"), lax.axis_size("req")
    n, width = hidden.shape
    model = w_query.shape[0]
    kvh = kv_cache.shape[2]
    kv = kv_cache.reshape(n, kv_cache.shape[1] * kvh, kv_cache.shape[3])
    lanes = kv.shape[1]
    i = np.arange(128) % (HEAD_SIZE // 2)
    freq = jnp.asarray((ROPE_BASE ** (-2.0 * i / HEAD_SIZE)).astype(np.float32)[None])
    ag, mg = attn_gain.reshape(-1, 128), moe_gain.reshape(-1, 128)
    ids, gates = expert_ids.T, expert_gates.T
    f = b = model // 2
    a = GATE_LANES + model - b
    gu = w_gateup.reshape(2 * model, w_gateup.shape[3])
    dn = w_down[0]
    bf, f32 = jnp.bfloat16, jnp.float32
    dma, v = pltpu.SemaphoreType.DMA, pltpu.VMEM
    k5 = NZ // 2 + 1
    args = (lengths, migrate, hidden, kv, ag, mg, freq, w_query, key_value_weight, output_weight, ids, gates, gu, dn)
    return pl.pallas_call(
        functools.partial(layer_kernel, n_tp, n_req),
        name="layer",
        out_shape=jax.ShapeDtypeStruct((n, width), bf),
        in_specs=[pl.BlockSpec(memory_space=pltpu.SMEM if i == 1 else pltpu.HBM) for i in range(len(args))],
        out_specs=pl.BlockSpec(memory_space=pltpu.VMEM),
        scratch_shapes=[
            pltpu.SMEM(lengths.shape, jnp.int32),
            v(hidden.shape, bf), v(ag.shape, f32), v(mg.shape, f32), v(freq.shape, f32), v(ids.shape, jnp.int32), v(gates.shape, f32),
            v(kv.shape, bf), v(w_query.shape, bf), v(key_value_weight.shape, bf), v(output_weight.shape, bf),
            v((2, n_tp, n, width), bf), v(kv.shape[1:], bf), v(kv.shape[1:], bf), v((n, model), bf), v((n_tp, n, model), bf),
            v((n, 8, 128), f32), v((n, 8, 128), f32), v((n, 8, 128), f32), v((8, lanes), f32),
            v((NZ, NY, n, a), bf), v((NZ, NY, n, b), bf), v((NZ, NY, n, f), f32), v((NZ, NY, n, f), f32),
            v((2,) + gu.shape, bf), v((512, 128), f32), v((2, model, 256), bf), v((2,) + dn.shape, bf),
            v((NZ, NY, n, f), bf), v((NZ, NY, n, f), bf),
            v((2, k5, NY, n, f), bf), v((2, k5, NY, n, f), bf), v((2, k5, n, f), bf), v((2, k5, n, f), bf),
            v((NY, n, f), bf), v((NY, n, f), bf), v((n_tp, n, width), bf), v((n_tp, n, width), bf), v((n_tp + 1, n, width), f32),
            dma((16,)), dma((n,)), dma((2 * n_tp,)), dma((2, n_tp)), dma, dma, dma((n_tp,)), dma((n_tp,)),
            dma((2,)), dma((2,)), dma((NY,)), dma((NY,)), dma((2, k5, NY)), dma((2, k5, NY)), dma((2, k5)), dma((2, k5)),
            dma((NZ, NY)), dma((NZ, NY)),
            dma((NZ, NY)), dma((NZ, NY)), dma((2, k5, NY)), dma((2, k5, NY)), dma((2, k5)), dma((2, k5)), dma((NY,)), dma((NY,)),
            dma((n_tp,)), dma((n_tp,)),
        ],
        compiler_params=pltpu.CompilerParams(collective_id=0, has_side_effects=True, vmem_limit_bytes=VMEM_LIMIT),
        cost_estimate=pl.CostEstimate(flops=1_500_000_000, bytes_accessed=16_000_000, transcendentals=1_000_000),
    )(*args)


def solution(mesh):
    placed = (
        P(("rep", "req"), "tp"),
        P(None, "req"),
        P("req"),
        P(("rep", "req"), None, "tp", None),
        P(),
        P(),
        P(None, "tp"),
        P(None, "tp"),
        P("tp", None),
        P(("rep", "req"), None, None, "tp"),
        P(("rep", "req"), "tp", None),
        P(("rep", "req"), None),
        P(("rep", "req"), None),
    )
    return jax.shard_map(
        layer, mesh=mesh, in_specs=placed, out_specs=P(("rep", "req"), "tp"), check_vma=False
    )
```

time: 174 us -> 77.7 us (0.45)
  blocking collectives: 97.8 us -> 0 us
  Pallas kernels: 23.1 us -> 75.5 us
  waiting for transfers between devices: 18.7 us -> 0 us
  local copies, waits for them, and re-layouts: 16 us -> 1.31 us
  between operations: 14.2 us -> 0.66 us
  matrix products: 1.97 us -> 0 us
    all_to_all x2 -> x0, blocking collectives: 97.8 us -> none  [the longest x1 51.9 us: shards(): lax.all_to_all(outbound, ('rep', 'req'), split_axis=0, concat_axis=0, til...]
    pallas_call x1, Pallas kernels: 23.1 us -> 75.5 us  [layer(): pl.pallas_call(functools.partial(layer_kernel, n_tp, n_req), name='layer'...]
    unnamed x2 -> x0, waiting for transfers between devices: 18.7 us -> none
    unnamed x20 -> x1, local copies, waits for them, and re-layouts: 9.12 us -> 1.31 us
    reshape x5 -> x0, local copies, waits for them, and re-layouts: 4.61 us -> none  [the longest x1 2.36 us: shards(): flattened = arrived_rows.reshape(-1, model_width)]
    dot_general x4 -> x0, matrix products: 1.97 us -> none  [the longest x1 0.56 us: shards(): jnp.dot(gate_table, returned_rows, precision=lax.Precision.HIGHEST, prefe...]
  transfers between devices with their start and end apart: 1 -> 0, of which waited for: 1 -> 0; matrix products, arithmetic and copies ran while one was open for 0% -> 0% of each run, Pallas kernels for 0% -> 0%
where the time goes in v3:
time: 77.7 us; the launch traced here: 77.5 us
  Pallas kernels  75.5 us (97%)
  local copies, waits for them, and re-layouts  1.31 us (2%)
    pallas_call x1, Pallas kernels, layer(): pl.pallas_call(functools.partial(layer_kernel, n_tp, n_req), name='layer'...  75.5 us

profile of v3, /device:TPU:8, one launch (start us, length us, event | category | flops | bytes accessed | tf_op | source)
XLA Modules:
  0.0 77.5 jit_solution(8666837539866507750)
XLA Ops:
  0.7 75.5 %layer.1 = bf16[16,384]{1,0:T(8,128)(2,1)} custom-call(s32[2,16]{1,0:T(2,128)} %len_h.1, s32[1]{0:T(128)S(6)} %copy.16.mig_s, bf16[16,384]{1,0:T(8,128)(2,1)} %hid_h.1, bf16[16,2048,128]{2,1,0:T(8,128)(2,1)} %bitcast.7, f32[12,128]{1,0:T(8,128)} %bitcast.10, f32[12,128]{1,0:T(8,128)} %bitcast.11, f32[1,128]{1,0:T(1,128)} %constant.2.clone.freq_h, ...), custom_call_target="tpu_custom_call" | custom-call | flops 1500000000 | bytes 16000000 | tf_op jit(solution)/shard_map/layer/pallas_call | solution.py:440
  76.2 1.3 %copy.17 = bf16[16,384]{1,0:T(8,128)(2,1)} copy(bf16[16,384]{1,0:T(8,128)(2,1)} %layer.1) | data formatting | bytes 24576

commit v4 on v3

--- a/solution.py
+++ b/solution.py
@@ -15,6 +15,7 @@
 GATE_LANES = 128
 NY, NZ = 4, 8
 VMEM_LIMIT = 58 * 2**20
+A_LANES, FA_LANES = 896, 768
 
 
 def rows_of(scalars, n):
@@ -59,8 +60,10 @@
     kvh = wkv_v.shape[1] // (2 * HEAD_SIZE)
     group = heads // kvh
     n_lanes = kv_v.shape[1]
-    a, b, f = ga.shape[-1], gb.shape[-1], pa.shape[-1]
+    a, b, fa, fb = ga.shape[-1], gb.shape[-1], pa.shape[-1], pb.shape[-1]
     opp = NZ // 2
+    part_b = (slice(0, b // 256 * 128), slice(b // 256 * 128, b))
+    part_fb = (slice(0, fb // 256 * 128), slice(fb // 256 * 128, fb))
     bf, f32 = jnp.bfloat16, jnp.float32
 
     def zc(k):
@@ -247,23 +250,17 @@
     REL = ((0, 1), (3, 2))
     AWAY = (1, 3, 2)
     for d in (0, 1):
-        send(ga.at[z, y], ga.at[z, y], a2_s.at[d, 1, 0], a2_r.at[d, 1, 0], nbr[d])
+        send(gb.at[z, y], gb.at[z, y], b1_s.at[d, 1], b1_r.at[d, 1], nbr[d])
     for k in AWAY:
         send(ga.at[z, y], ga.at[z, y], a1_s.at[k], a1_r.at[y], at(yc(k), z))
     for d in (0, 1):
-        send(gb.at[z, y], gb.at[z, y], b1_s.at[d, 1], b1_r.at[d, 1], nbr[d])
+        send(ga.at[z, y], ga.at[z, y], a2_s.at[d, 1, 0], a2_r.at[d, 1, 0], nbr[d])
     for k in AWAY:
         send(gb.at[z, y], gb.at[z, y], b2_s.at[0, k], b2_r.at[z, y], at(yc(k), z))
     own = jnp.zeros((n, width), f32)
     for t in range(n_tp):
         own = jnp.where(tp == t, total[:, t * width:(t + 1) * width], own)
     xf[n_tp] = own
-    for k in AWAY:
-        yb = yc(k)
-        took(ga.at[z, yb], a1_s.at[k], a1_r.at[yb], at(yb, z))
-        for d in (0, 1):
-            send(ga.at[z, yb], ga.at[z, yb], a2_s.at[d, 1, k], a2_r.at[d, 1, k], nbr[d])
-
     number = (rep * n_req + req, (1 - rep) * n_req + req)
 
     def compute(zs):
@@ -281,14 +278,16 @@
         o = jnp.dot(acts[0], dn[0], preferred_element_type=f32) + jnp.dot(acts[1], dn[1], preferred_element_type=f32)
         for i, zz in enumerate(zs):
             block = o[i * NY * n:(i + 1) * NY * n]
-            pa[zz] = block[:, 0:f].reshape(NY, n, f)
-            pb[zz] = block[:, f:2 * f].reshape(NY, n, f)
-            by_s[zz] = block[:, f:2 * f].astype(bf).reshape(NY, n, f)
+            pa[zz] = block[:, 0:fa].reshape(NY, n, fa)
+            pb[zz] = block[:, fa:].reshape(NY, n, fb)
+            by_s[zz] = block[:, fa:].astype(bf).reshape(NY, n, fb)
             for k in AWAY:
                 send(by_s.at[zz, yc(k)], by_r.at[zz, y], rby_s.at[zz, k], rby_r.at[zz, y], at(yc(k), z))
 
-    def chunk(s):
-        zs = [zc(s)] if s in (0, opp) else [zc(-s), zc(s)]
+    def chunks(*steps):
+        zs = []
+        for s in steps:
+            zs += [zc(s)] if s in (0, opp) else [zc(-s), zc(s)]
         for zz in zs:
             for k in AWAY:
                 took(gb.at[zz, yc(k)], b2_s.at[0, k], b2_r.at[zz, yc(k)], at(yc(k), z))
@@ -302,38 +301,51 @@
         took(ra.at[d, k, i], rsa_s.at[d, k, i], rsa_r.at[d, k, i], nbr[d])
         return ra[d, k, i].astype(f32)
 
-    h = b // 2
-    for s in range(1, opp + 1):
+    def pass_b(s):
         for d in (0, 1):
             zz = zc(-s) if d == 0 else zc(s)
             if s < opp:
                 took(gb.at[zz, y], b1_s.at[d, s], b1_r.at[d, s], nbr[d])
-                block = gb.at[zz, y] if s + 1 < opp else gb.at[zz, y, :, d * h:(d + 1) * h]
+                block = gb.at[zz, y] if s + 1 < opp else gb.at[zz, y, :, part_b[d]]
                 send(block, block, b1_s.at[d, s + 1], b1_r.at[d, s + 1], nbr[d])
             else:
-                block = gb.at[zz, y, :, d * h:(d + 1) * h]
-                took(block, b1_s.at[d, s], b1_r.at[d, s], nbr[d])
-            if s < opp or d == 1:
-                for k in AWAY:
-                    send(gb.at[zz, y], gb.at[zz, y], b2_s.at[2 * s - 1 + d if s < opp else 2 * s - 1, k], b2_r.at[zz, y], at(yc(k), z))
-        if s == opp:
-            chunk(2)
-            chunk(3)
-            for d in (0, 1):
-                for i in REL[1 - d]:
-                    a_send(d, opp - 1, i, pa[zc(opp - 1) if d == 0 else zc(1 - opp), yc(i)])
+                took(gb.at[zz, y, :, part_b[d]], b1_s.at[d, s], b1_r.at[d, s], nbr[d])
+        for d in (0, 1) if s < opp else (0,):
+            zz = zc(-s) if d == 0 else zc(s)
+            for k in AWAY:
+                send(gb.at[zz, y], gb.at[zz, y], b2_s.at[2 * s - 1 + d, k], b2_r.at[zz, y], at(yc(k), z))
+
+    def pass_a(s):
         for i in ORDER:
             for d in (0, 1):
                 if s == opp and i not in REL[d]:
                     continue
                 zz = zc(-s) if d == 0 else zc(s)
                 yb = yc(i)
-                took(ga.at[zz, yb], a2_s.at[d, s, i], a2_r.at[d, s, i], nbr[d])
+                if s:
+                    took(ga.at[zz, yb], a2_s.at[d, s, i], a2_r.at[d, s, i], nbr[d])
+                elif i == 0:
+                    continue
+                elif d == 0:
+                    took(ga.at[z, yb], a1_s.at[i], a1_r.at[yb], at(yb, z))
                 if s + 1 < opp or (s + 1 == opp and i in REL[d]):
                     send(ga.at[zz, yb], ga.at[zz, yb], a2_s.at[d, s + 1, i], a2_r.at[d, s + 1, i], nbr[d])
-        if s in (2, 3):
-            chunk(s - 2)
-    chunk(opp)
+
+    pass_b(1)
+    pass_a(0)
+    pass_b(2)
+    pass_a(1)
+    pass_b(3)
+    pass_a(2)
+    pass_b(4)
+    chunks(0, 1)
+    pass_a(3)
+    chunks(2, 3)
+    for d in (0, 1):
+        for i in REL[1 - d]:
+            a_send(d, opp - 1, i, pa[zc(opp - 1) if d == 0 else zc(1 - opp), yc(i)])
+    pass_a(4)
+    chunks(4)
 
     def a_step(k):
         for i in ORDER:
@@ -352,23 +364,21 @@
             value = value + by_r[zz, yc(k)].astype(f32)
         return value
 
-    e = f // 2
-
     def b_step(k):
         if k == opp:
             value = b_own(zc(k)).astype(bf)
             for d in (0, 1):
-                lanes = slice(d * e, (d + 1) * e)
+                lanes = part_fb[d]
                 sb[d, k, :, lanes] = value[:, lanes]
                 send(sb.at[d, k, :, lanes], rb.at[d, k, :, lanes], rsb_s.at[d, k], rsb_r.at[d, k], nbr[d])
             return
         for d in (0, 1):
             value = b_own(zc(k) if d == 0 else zc(-k))
             if k == opp - 1:
-                lanes = slice(d * e, (d + 1) * e)
+                lanes = part_fb[d]
                 took(rb.at[d, k + 1, :, lanes], rsb_s.at[d, k + 1], rsb_r.at[d, k + 1], nbr[d])
                 added = value[:, lanes] + rb[d, k + 1, :, lanes].astype(f32)
-                value = jnp.concatenate([added, value[:, e:]] if d == 0 else [value[:, :e], added], axis=1)
+                value = jnp.concatenate([added, value[:, part_fb[1]]] if d == 0 else [value[:, part_fb[0]], added], axis=1)
             else:
                 took(rb.at[d, k + 1], rsb_s.at[d, k + 1], rsb_r.at[d, k + 1], nbr[d])
                 value = value + rb[d, k + 1].astype(f32)
@@ -429,8 +439,8 @@
     freq = jnp.asarray((ROPE_BASE ** (-2.0 * i / HEAD_SIZE)).astype(np.float32)[None])
     ag, mg = attn_gain.reshape(-1, 128), moe_gain.reshape(-1, 128)
     ids, gates = expert_ids.T, expert_gates.T
-    f = b = model // 2
-    a = GATE_LANES + model - b
+    a, fa = A_LANES, FA_LANES
+    b, fb = GATE_LANES + model - a, model - fa
     gu = w_gateup.reshape(2 * model, w_gateup.shape[3])
     dn = w_down[0]
     bf, f32 = jnp.bfloat16, jnp.float32
@@ -449,11 +459,11 @@
             v(kv.shape, bf), v(w_query.shape, bf), v(key_value_weight.shape, bf), v(output_weight.shape, bf),
             v((2, n_tp, n, width), bf), v(kv.shape[1:], bf), v(kv.shape[1:], bf), v((n, model), bf), v((n_tp, n, model), bf),
             v((n, 8, 128), f32), v((n, 8, 128), f32), v((n, 8, 128), f32), v((8, lanes), f32),
-            v((NZ, NY, n, a), bf), v((NZ, NY, n, b), bf), v((NZ, NY, n, f), f32), v((NZ, NY, n, f), f32),
+            v((NZ, NY, n, a), bf), v((NZ, NY, n, b), bf), v((NZ, NY, n, fa), f32), v((NZ, NY, n, fb), f32),
             v((2,) + gu.shape, bf), v((512, 128), f32), v((2, model, 256), bf), v((2,) + dn.shape, bf),
-            v((NZ, NY, n, f), bf), v((NZ, NY, n, f), bf),
-            v((2, k5, NY, n, f), bf), v((2, k5, NY, n, f), bf), v((2, k5, n, f), bf), v((2, k5, n, f), bf),
-            v((NY, n, f), bf), v((NY, n, f), bf), v((n_tp, n, width), bf), v((n_tp, n, width), bf), v((n_tp + 1, n, width), f32),
+            v((NZ, NY, n, fb), bf), v((NZ, NY, n, fb), bf),
+            v((2, k5, NY, n, fa), bf), v((2, k5, NY, n, fa), bf), v((2, k5, n, fb), bf), v((2, k5, n, fb), bf),
+            v((NY, n, fa), bf), v((NY, n, fa), bf), v((n_tp, n, width), bf), v((n_tp, n, width), bf), v((n_tp + 1, n, width), f32),
             dma((16,)), dma((n,)), dma((2 * n_tp,)), dma((2, n_tp)), dma, dma, dma((n_tp,)), dma((n_tp,)),
             dma((2,)), dma((2,)), dma((NY,)), dma((NY,)), dma((2, k5, NY)), dma((2, k5, NY)), dma((2, k5)), dma((2, k5)),
             dma((NZ, NY)), dma((NZ, NY)),

time: 77.7 us -> 75 us (0.965)
  Pallas kernels: 75.5 us -> 72.9 us
    pallas_call x1, Pallas kernels: 75.5 us -> 72.9 us  [layer(): pl.pallas_call(functools.partial(layer_kernel, n_tp, n_req), name='layer'...]
where the time goes in v4:
time: 75 us; the launch traced here: 74.9 us
  Pallas kernels  72.9 us (97%)
  local copies, waits for them, and re-layouts  1.31 us (2%)
    pallas_call x1, Pallas kernels, layer(): pl.pallas_call(functools.partial(layer_kernel, n_tp, n_req), name='layer'...  72.9 us

profile of v4, /device:TPU:8, one launch (start us, length us, event | category | flops | bytes accessed | tf_op | source)
XLA Modules:
  0.0 74.9 jit_solution(17352215778106157373)
XLA Ops:
  0.7 72.9 %layer.1 = bf16[16,384]{1,0:T(8,128)(2,1)} custom-call(s32[2,16]{1,0:T(2,128)} %len_h.1, s32[1]{0:T(128)S(6)} %copy.16.mig_s, bf16[16,384]{1,0:T(8,128)(2,1)} %hid_h.1, bf16[16,2048,128]{2,1,0:T(8,128)(2,1)} %bitcast.7, f32[12,128]{1,0:T(8,128)} %bitcast.10, f32[12,128]{1,0:T(8,128)} %bitcast.11, f32[1,128]{1,0:T(1,128)} %constant.2.clone.freq_h, ...), custom_call_target="tpu_custom_call" | custom-call | flops 1500000000 | bytes 16000000 | tf_op jit(solution)/shard_map/layer/pallas_call | solution.py:450
  73.5 1.3 %copy.17 = bf16[16,384]{1,0:T(8,128)(2,1)} copy(bf16[16,384]{1,0:T(8,128)(2,1)} %layer.1) | data formatting | bytes 24576

commit v5 on v4

--- a/solution.py
+++ b/solution.py
@@ -26,19 +26,22 @@
     return out
 
 
-def attend(q, kvn, kv, bias, limit):
+def attend(requests, bias):
     scale = HEAD_SIZE ** (-0.5)
-    s = lax.dot_general(q.astype(jnp.bfloat16), kv, (((1,), (1,)), ((), ())), preferred_element_type=jnp.float32)
-    lane = lax.broadcasted_iota(jnp.int32, s.shape, 1)
-    s = jnp.where(lane < limit, s * scale + bias, MASKED)
-    own = jnp.sum(q * kvn, axis=1, keepdims=True) * scale
-    peak = jnp.maximum(jnp.max(s, axis=1, keepdims=True), own)
+    scores, owns = [], []
+    for q, kvn, kv, limit in requests:
+        s = lax.dot_general(q.astype(jnp.bfloat16), kv, (((1,), (1,)), ((), ())), preferred_element_type=jnp.float32)
+        place = lax.broadcasted_iota(jnp.int32, s.shape, 1)
+        scores.append(jnp.where(place < limit, s * scale + bias, MASKED)[None])
+        owns.append((jnp.sum(q * kvn, axis=1, keepdims=True) * scale)[None])
+    s, own = jnp.concatenate(scores, axis=0), jnp.concatenate(owns, axis=0)
+    peak = jnp.maximum(jnp.max(s, axis=2, keepdims=True), own)
     p = jnp.exp(s - peak)
     p_own = jnp.exp(own - peak)
-    inv = 1.0 / (jnp.sum(p, axis=1, keepdims=True) + p_own)
+    inv = 1.0 / (jnp.sum(p, axis=2, keepdims=True) + p_own)
     w = (p * inv).astype(jnp.bfloat16)
     w_own = (p_own * inv).astype(jnp.bfloat16).astype(jnp.float32)
-    return jnp.dot(w, kv, preferred_element_type=jnp.float32) + w_own * kvn
+    return [jnp.dot(w[g], kv, preferred_element_type=jnp.float32) + w_own[g] * kvn for g, (q, kvn, kv, limit) in enumerate(requests)]
 
 
 def layer_kernel(
@@ -143,8 +146,8 @@
         turned = jnp.where(first, -pltpu.roll(v, 128 - half, 1), pltpu.roll(v, half, 1))
         return v * cosine + turned * sine
 
-    head = lax.broadcasted_iota(jnp.int32, (8, n_lanes), 0)
-    pos = lax.broadcasted_iota(jnp.int32, (8, n_lanes), 1)
+    head = lax.broadcasted_iota(jnp.int32, bias_s.shape, 0)
+    pos = lax.broadcasted_iota(jnp.int32, bias_s.shape, 1)
     bias_s[...] = jnp.where(lax.rem(pos, kvh) == head // group, 0.0, MASKED)
 
     eye = lax.broadcasted_iota(jnp.int32, (n, n), 0) == lax.broadcasted_iota(jnp.int32, (n, n), 1)
@@ -201,21 +204,25 @@
     kv_copy = rcopy(kv_send, kv_recv, kv_send_sem, kv_recv_sem, partner)
     kv_copy.start()
 
-    def one(r):
-        limit = kvh * jnp.where(rep == 0, len_s[0, r], len_s[1, r])
-        ctx_s[r] = attend(q_s[r], kvn_s[r], kv_v[r], bias_s[...], limit)
-
-    UNROLL = 4
+    def own_request(r):
+        return q_s[r], kvn_s[r], kv_v[r], kvh * jnp.where(rep == 0, len_s[0, r], len_s[1, r])
+
+    GROUP = 8
 
     def step(i, carry):
-        for j in range(UNROLL):
-            one(i * UNROLL + j)
+        rs = [i * GROUP + j for j in range(GROUP)]
+        for r, o in zip(rs, attend([own_request(r) for r in rs], bias_s[...])):
+            ctx_s[r] = o
         return carry
 
-    lax.fori_loop(0, n // UNROLL, step, 0)
+    lax.fori_loop(0, n // GROUP - 1, step, 0)
     kv_copy.wait()
+    rs = list(range(n - GROUP, n))
     limit = kvh * jnp.where(rep == 0, len_s[1, slot], len_s[0, slot])
-    arrived = attend(q_s[slot], kvn_s[slot], kv_recv[...], bias_s[...], limit)
+    last = attend([own_request(r) for r in rs] + [(q_s[slot], kvn_s[slot], kv_recv[...], limit)], bias_s[...])
+    for r, o in zip(rs, last):
+        ctx_s[r] = o
+    arrived = last[-1]
 
     blocks = []
     for i in range(heads // 2):

time: 75 us -> 69.9 us (0.932)
  Pallas kernels: 72.9 us -> 67.7 us
    pallas_call x1, Pallas kernels: 72.9 us -> 67.7 us  [layer(): pl.pallas_call(functools.partial(layer_kernel, n_tp, n_req), name='layer'...]
where the time goes in v5:
time: 69.9 us; the launch traced here: 69.7 us
  Pallas kernels  67.7 us (97%)
  local copies, waits for them, and re-layouts  1.31 us (2%)
    pallas_call x1, Pallas kernels, layer(): pl.pallas_call(functools.partial(layer_kernel, n_tp, n_req), name='layer'...  67.7 us

profile of v5, /device:TPU:8, one launch (start us, length us, event | category | flops | bytes accessed | tf_op | source)
XLA Modules:
  0.0 69.7 jit_solution(5345019122773393853)
XLA Ops:
  0.7 67.7 %layer.1 = bf16[16,384]{1,0:T(8,128)(2,1)} custom-call(s32[2,16]{1,0:T(2,128)} %len_h.1, s32[1]{0:T(128)S(6)} %copy.16.mig_s, bf16[16,384]{1,0:T(8,128)(2,1)} %hid_h.1, bf16[16,2048,128]{2,1,0:T(8,128)(2,1)} %bitcast.7, f32[12,128]{1,0:T(8,128)} %bitcast.10, f32[12,128]{1,0:T(8,128)} %bitcast.11, f32[1,128]{1,0:T(1,128)} %constant.2.clone.freq_h, ...), custom_call_target="tpu_custom_call" | custom-call | flops 1500000000 | bytes 16000000 | tf_op jit(solution)/shard_map/layer/pallas_call | solution.py:457
  68.4 1.3 %copy.17 = bf16[16,384]{1,0:T(8,128)(2,1)} copy(bf16[16,384]{1,0:T(8,128)(2,1)} %layer.1) | data formatting | bytes 24576

commit v6 on v5

--- a/solution.py
+++ b/solution.py
@@ -83,15 +83,15 @@
 
     nbr = (at(y, zc(1)), at(y, zc(-1)))
     partner = {"rep": 1 - rep}
-    pending = []
 
     def rcopy(src, dst, ssem, rsem, dev):
         return pltpu.make_async_remote_copy(src_ref=src, dst_ref=dst, send_sem=ssem, recv_sem=rsem, device_id=dev, device_id_type=MESH)
 
     def send(*args):
-        c = rcopy(*args)
-        c.start()
-        pending.append(c)
+        rcopy(*args).start()
+
+    def sent(blocks, ssem):
+        rcopy(blocks, blocks, ssem, ssem, partner).wait_send()
 
     def took(dst, ssem, rsem, dev):
         rcopy(dst, dst, ssem, rsem, dev).wait_recv()
@@ -106,9 +106,8 @@
 
     small = [load(*p) for p in ((hid_h, hid), (len_h, len_s), (ids_h, ids), (gates_h, gates), (freq_h, freq), (ag_h, ag), (mg_h, mg))]
     proj = [load(wq_h, wq_v), load(wkv_h, wkv_v)]
-    kv_loads = [pltpu.make_async_copy(kv_h.at[r], kv_v.at[r], kv_sem.at[r]) for r in range(n)]
-    for c in kv_loads:
-        c.start()
+    for r in range(n):
+        pltpu.make_async_copy(kv_h.at[r], kv_v.at[r], kv_sem).start()
     load_o = load(wo_h, wo_v)
     own_gu = load(gu_h, raw.at[0])
     own_dn = load(dn_h, dn.at[0])
@@ -124,8 +123,8 @@
 
     for c in small:
         c.wait()
-    for i, (side, t) in enumerate(peers):
-        send(hid, tok.at[side, tp], tok_send_sem.at[i], tok_recv_sem.at[side, tp], {"rep": far_rep(side), "tp": t})
+    for side, t in peers:
+        send(hid, tok.at[side, tp], tok_send_sem.at[side], tok_recv_sem.at[side], {"rep": far_rep(side), "tp": t})
     tok[0, tp] = hid[...]
     send(gu_h, raw.at[1], wx_s.at[0], wx_r.at[0], partner)
     send(dn_h, dn.at[1], wx_s.at[1], wx_r.at[1], partner)
@@ -172,8 +171,8 @@
             return carry
         lax.fori_loop(0, raw.shape[1] // part, step, 0)
 
-    for side, t in peers:
-        took(tok.at[side, t], tok_send_sem.at[0], tok_recv_sem.at[side, t], {"tp": t})
+    took(tok.at[0, 0:n_tp - 1], tok_send_sem.at[0], tok_recv_sem.at[0], partner)
+    took(tok.at[1], tok_send_sem.at[1], tok_recv_sem.at[1], partner)
 
     moved_w = lax.broadcasted_iota(jnp.int32, (n, width), 0) == slot
     tokens = jnp.concatenate(
@@ -198,8 +197,7 @@
         for h in range(g * group, (g + 1) * group):
             kvn_s[:, h, :] = both
 
-    for c in kv_loads:
-        c.wait()
+    pltpu.make_async_copy(kv_h, kv_v, kv_sem).wait()
     kv_send[...] = kv_v[slot]
     kv_copy = rcopy(kv_send, kv_recv, kv_send_sem, kv_recv_sem, partner)
     kv_copy.start()
@@ -234,7 +232,7 @@
     partial = jnp.dot(context, wo_v[...], preferred_element_type=f32)
     part_send[...] = partial.astype(bf)
     for k in (1, 3, 2):
-        send(part_send, part_recv.at[tp], part_send_sem.at[k], part_recv_sem.at[tp], {"tp": tc(k)})
+        send(part_send, part_recv.at[tp], part_send_sem, part_recv_sem, {"tp": tc(k)})
     own_gu.wait()
     own_dn.wait()
     split(0)
@@ -242,10 +240,9 @@
     took(dn.at[1], wx_s.at[1], wx_r.at[1], partner)
     split(1)
     total = tokens + partial
+    took(part_recv.at[0:n_tp - 1], part_send_sem, part_recv_sem, partner)
     for k in (1, 3, 2):
-        t = tc(k)
-        took(part_recv.at[t], part_send_sem.at[k], part_recv_sem.at[t], {"tp": t})
-        total = total + part_recv[t].astype(f32)
+        total = total + part_recv[tc(k)].astype(f32)
     mean = jnp.mean(total * total, axis=1, keepdims=True)
     gain = jnp.concatenate([mg[i:i + 1, :] for i in range(mg.shape[0])], axis=1)
     x = (total * lax.rsqrt(mean + EPSILON) * gain).astype(bf)
@@ -257,13 +254,13 @@
     REL = ((0, 1), (3, 2))
     AWAY = (1, 3, 2)
     for d in (0, 1):
-        send(gb.at[z, y], gb.at[z, y], b1_s.at[d, 1], b1_r.at[d, 1], nbr[d])
+        send(gb.at[z, y], gb.at[z, y], b1_s.at[0], b1_r.at[d, 1], nbr[d])
     for k in AWAY:
-        send(ga.at[z, y], ga.at[z, y], a1_s.at[k], a1_r.at[y], at(yc(k), z))
+        send(ga.at[z, y], ga.at[z, y], a1_s, a1_r.at[y], at(yc(k), z))
     for d in (0, 1):
-        send(ga.at[z, y], ga.at[z, y], a2_s.at[d, 1, 0], a2_r.at[d, 1, 0], nbr[d])
+        send(ga.at[z, y], ga.at[z, y], a2_s, a2_r.at[d, 1, 0], nbr[d])
     for k in AWAY:
-        send(gb.at[z, y], gb.at[z, y], b2_s.at[0, k], b2_r.at[z, y], at(yc(k), z))
+        send(gb.at[z, y], gb.at[z, y], b2_s, b2_r.at[z], at(yc(k), z))
     own = jnp.zeros((n, width), f32)
     for t in range(n_tp):
         own = jnp.where(tp == t, total[:, t * width:(t + 1) * width], own)
@@ -289,38 +286,37 @@
             pb[zz] = block[:, fa:].reshape(NY, n, fb)
             by_s[zz] = block[:, fa:].astype(bf).reshape(NY, n, fb)
             for k in AWAY:
-                send(by_s.at[zz, yc(k)], by_r.at[zz, y], rby_s.at[zz, k], rby_r.at[zz, y], at(yc(k), z))
+                send(by_s.at[zz, yc(k)], by_r.at[zz, y], rby_s, rby_r.at[zz], at(yc(k), z))
 
     def chunks(*steps):
         zs = []
         for s in steps:
             zs += [zc(s)] if s in (0, opp) else [zc(-s), zc(s)]
         for zz in zs:
-            for k in AWAY:
-                took(gb.at[zz, yc(k)], b2_s.at[0, k], b2_r.at[zz, yc(k)], at(yc(k), z))
+            took(gb.at[zz, 0:NY - 1], b2_s, b2_r.at[zz], partner)
         compute(zs)
 
     def a_send(d, k, i, value):
-        sa[d, k, i] = value.astype(bf)
-        send(sa.at[d, k, i], ra.at[d, k, i], rsa_s.at[d, k, i], rsa_r.at[d, k, i], nbr[d])
+        sa[d * (opp + 1) + k, i] = value.astype(bf)
+        send(sa.at[d * (opp + 1) + k, i], ra.at[d, k, i], rsa_s, rsa_r.at[d, k, i], nbr[d])
 
     def a_took(d, k, i):
-        took(ra.at[d, k, i], rsa_s.at[d, k, i], rsa_r.at[d, k, i], nbr[d])
+        took(ra.at[d, k, i], rsa_s, rsa_r.at[d, k, i], nbr[d])
         return ra[d, k, i].astype(f32)
 
     def pass_b(s):
         for d in (0, 1):
             zz = zc(-s) if d == 0 else zc(s)
             if s < opp:
-                took(gb.at[zz, y], b1_s.at[d, s], b1_r.at[d, s], nbr[d])
+                took(gb.at[zz, y], b1_s.at[0], b1_r.at[d, s], nbr[d])
                 block = gb.at[zz, y] if s + 1 < opp else gb.at[zz, y, :, part_b[d]]
-                send(block, block, b1_s.at[d, s + 1], b1_r.at[d, s + 1], nbr[d])
+                send(block, block, b1_s.at[0 if s + 1 < opp else 1], b1_r.at[d, s + 1], nbr[d])
             else:
-                took(gb.at[zz, y, :, part_b[d]], b1_s.at[d, s], b1_r.at[d, s], nbr[d])
+                took(gb.at[zz, y, :, part_b[d]], b1_s.at[0], b1_r.at[d, s], nbr[d])
         for d in (0, 1) if s < opp else (0,):
             zz = zc(-s) if d == 0 else zc(s)
             for k in AWAY:
-                send(gb.at[zz, y], gb.at[zz, y], b2_s.at[2 * s - 1 + d, k], b2_r.at[zz, y], at(yc(k), z))
+                send(gb.at[zz, y], gb.at[zz, y], b2_s, b2_r.at[zz], at(yc(k), z))
 
     def pass_a(s):
         for i in ORDER:
@@ -330,13 +326,13 @@
                 zz = zc(-s) if d == 0 else zc(s)
                 yb = yc(i)
                 if s:
-                    took(ga.at[zz, yb], a2_s.at[d, s, i], a2_r.at[d, s, i], nbr[d])
+                    took(ga.at[zz, yb], a2_s, a2_r.at[d, s, i], nbr[d])
                 elif i == 0:
                     continue
                 elif d == 0:
-                    took(ga.at[z, yb], a1_s.at[i], a1_r.at[yb], at(yb, z))
+                    took(ga.at[z, yb], a1_s, a1_r.at[yb], at(yb, z))
                 if s + 1 < opp or (s + 1 == opp and i in REL[d]):
-                    send(ga.at[zz, yb], ga.at[zz, yb], a2_s.at[d, s + 1, i], a2_r.at[d, s + 1, i], nbr[d])
+                    send(ga.at[zz, yb], ga.at[zz, yb], a2_s, a2_r.at[d, s + 1, i], nbr[d])
 
     pass_b(1)
     pass_a(0)
@@ -366,8 +362,8 @@
 
     def b_own(zz):
         value = pb[zz, y]
+        took(by_r.at[zz, 0:NY - 1], rby_s, rby_r.at[zz], partner)
         for k in AWAY:
-            took(by_r.at[zz, yc(k)], rby_s.at[zz, k], rby_r.at[zz, yc(k)], at(yc(k), z))
             value = value + by_r[zz, yc(k)].astype(f32)
         return value
 
@@ -377,20 +373,20 @@
             for d in (0, 1):
                 lanes = part_fb[d]
                 sb[d, k, :, lanes] = value[:, lanes]
-                send(sb.at[d, k, :, lanes], rb.at[d, k, :, lanes], rsb_s.at[d, k], rsb_r.at[d, k], nbr[d])
+                send(sb.at[d, k, :, lanes], rb.at[d, k, :, lanes], rsb_s.at[1], rsb_r.at[d, k], nbr[d])
             return
         for d in (0, 1):
             value = b_own(zc(k) if d == 0 else zc(-k))
             if k == opp - 1:
                 lanes = part_fb[d]
-                took(rb.at[d, k + 1, :, lanes], rsb_s.at[d, k + 1], rsb_r.at[d, k + 1], nbr[d])
+                took(rb.at[d, k + 1, :, lanes], rsb_s.at[0], rsb_r.at[d, k + 1], nbr[d])
                 added = value[:, lanes] + rb[d, k + 1, :, lanes].astype(f32)
                 value = jnp.concatenate([added, value[:, part_fb[1]]] if d == 0 else [value[:, part_fb[0]], added], axis=1)
             else:
-                took(rb.at[d, k + 1], rsb_s.at[d, k + 1], rsb_r.at[d, k + 1], nbr[d])
+                took(rb.at[d, k + 1], rsb_s.at[0], rsb_r.at[d, k + 1], nbr[d])
                 value = value + rb[d, k + 1].astype(f32)
             sb[d, k] = value.astype(bf)
-            send(sb.at[d, k], rb.at[d, k], rsb_s.at[d, k], rsb_r.at[d, k], nbr[d])
+            send(sb.at[d, k], rb.at[d, k], rsb_s.at[0], rsb_r.at[d, k], nbr[d])
 
     a_step(4)
     a_step(3)
@@ -402,17 +398,16 @@
     for k in AWAY:
         yb = yc(k)
         ys[yb] = (pa[z, yb] + a_took(0, 1, k) + a_took(1, 1, k)).astype(bf)
-        send(ys.at[yb], yr.at[y], ry_s.at[k], ry_r.at[y], at(yb, z))
+        send(ys.at[yb], yr.at[y], ry_s, ry_r, at(yb, z))
     total_a = pa[z, y] + a_took(0, 1, 0) + a_took(1, 1, 0)
     b_step(1)
     total_b = b_own(z)
     for d in (0, 1):
-        took(rb.at[d, 1], rsb_s.at[d, 1], rsb_r.at[d, 1], nbr[d])
+        took(rb.at[d, 1], rsb_s.at[0], rsb_r.at[d, 1], nbr[d])
         total_b = total_b + rb[d, 1].astype(f32)
+    took(yr.at[0:NY - 1], ry_s, ry_r, partner)
     for k in AWAY:
-        yb = yc(k)
-        took(yr.at[yb], ry_s.at[k], ry_r.at[yb], at(yb, z))
-        total_a = total_a + yr[yb].astype(f32)
+        total_a = total_a + yr[yc(k)].astype(f32)
 
     total = jnp.concatenate([total_a, total_b], axis=1)
     for t in range(n_tp):
@@ -421,15 +416,28 @@
         xs[t] = quarter.astype(bf)
     for k in AWAY:
         t = tc(k)
-        send(xs.at[t], xr.at[tp], rx_s.at[k], rx_r.at[tp], {"tp": t})
+        send(xs.at[t], xr.at[tp], rx_s, rx_r, {"tp": t})
     value = xf[n_tp] + xf[tp]
+    took(xr.at[0:n_tp - 1], rx_s, rx_r, partner)
     for k in AWAY:
-        t = tc(k)
-        took(xr.at[t], rx_s.at[k], rx_r.at[t], {"tp": t})
-        value = value + xr[t].astype(f32)
+        value = value + xr[tc(k)].astype(f32)
     out[...] = value.astype(bf)
-    for c in pending:
-        c.wait_send()
+    sent(tok.at[0, 0:n_tp - 1], tok_send_sem.at[0])
+    sent(tok.at[1], tok_send_sem.at[1])
+    sent(raw.at[0], wx_s.at[0])
+    sent(dn.at[0], wx_s.at[1])
+    sent(part_recv.at[0:n_tp - 1], part_send_sem)
+    sent(ga.at[0, 0:NY - 1], a1_s)
+    sent(ga.at[0:NZ - 1], a2_s)
+    sent(gb.at[0:opp - 1, 0:2], b1_s.at[0])
+    sent(gb.at[0, 0], b1_s.at[1])
+    sent(gb.at[0:NZ - 2], b2_s)
+    sent(by_s.at[0:NZ - 2], rby_s)
+    sent(sa.at[0:NZ - 1], rsa_s)
+    sent(sb.at[:, 0:opp - 1], rsb_s.at[0])
+    sent(sb.at[0, 0], rsb_s.at[1])
+    sent(ys.at[0:NY - 1], ry_s)
+    sent(xs.at[0:n_tp - 1], rx_s)
 
 
 def layer(
@@ -469,13 +477,11 @@
             v((NZ, NY, n, a), bf), v((NZ, NY, n, b), bf), v((NZ, NY, n, fa), f32), v((NZ, NY, n, fb), f32),
             v((2,) + gu.shape, bf), v((512, 128), f32), v((2, model, 256), bf), v((2,) + dn.shape, bf),
             v((NZ, NY, n, fb), bf), v((NZ, NY, n, fb), bf),
-            v((2, k5, NY, n, fa), bf), v((2, k5, NY, n, fa), bf), v((2, k5, n, fb), bf), v((2, k5, n, fb), bf),
+            v((2 * k5, NY, n, fa), bf), v((2, k5, NY, n, fa), bf), v((2, k5, n, fb), bf), v((2, k5, n, fb), bf),
             v((NY, n, fa), bf), v((NY, n, fa), bf), v((n_tp, n, width), bf), v((n_tp, n, width), bf), v((n_tp + 1, n, width), f32),
-            dma((16,)), dma((n,)), dma((2 * n_tp,)), dma((2, n_tp)), dma, dma, dma((n_tp,)), dma((n_tp,)),
-            dma((2,)), dma((2,)), dma((NY,)), dma((NY,)), dma((2, k5, NY)), dma((2, k5, NY)), dma((2, k5)), dma((2, k5)),
-            dma((NZ, NY)), dma((NZ, NY)),
-            dma((NZ, NY)), dma((NZ, NY)), dma((2, k5, NY)), dma((2, k5, NY)), dma((2, k5)), dma((2, k5)), dma((NY,)), dma((NY,)),
-            dma((n_tp,)), dma((n_tp,)),
+            dma((12,)), dma, dma((2,)), dma((2,)), dma, dma, dma, dma,
+            dma((2,)), dma((2,)), dma, dma((NY,)), dma, dma((2, k5, NY)), dma((2,)), dma((2, k5)), dma, dma((NZ,)),
+            dma, dma((NZ,)), dma, dma((2, k5, NY)), dma((2,)), dma((2, k5)), dma, dma, dma, dma,
         ],
         compiler_params=pltpu.CompilerParams(collective_id=0, has_side_effects=True, vmem_limit_bytes=VMEM_LIMIT),
         cost_estimate=pl.CostEstimate(flops=1_500_000_000, bytes_accessed=16_000_000, transcendentals=1_000_000),

time: 69.9 us -> 67.4 us (0.964)
  Pallas kernels: 67.7 us -> 65.3 us
    pallas_call x1, Pallas kernels: 67.7 us -> 65.3 us  [layer(): pl.pallas_call(functools.partial(layer_kernel, n_tp, n_req), name='layer'...]
where the time goes in v6:
time: 67.4 us; the launch traced here: 67.2 us
  Pallas kernels  65.3 us (97%)
  local copies, waits for them, and re-layouts  1.31 us (2%)
    pallas_call x1, Pallas kernels, layer(): pl.pallas_call(functools.partial(layer_kernel, n_tp, n_req), name='layer'...  65.3 us

profile of v6, /device:TPU:8, one launch (start us, length us, event | category | flops | bytes accessed | tf_op | source)
XLA Modules:
  0.0 67.2 jit_solution(14247330944771090629)
XLA Ops:
  0.7 65.3 %layer.1 = bf16[16,384]{1,0:T(8,128)(2,1)} custom-call(s32[2,16]{1,0:T(2,128)} %len_h.1, s32[1]{0:T(128)S(6)} %copy.16.mig_s, bf16[16,384]{1,0:T(8,128)(2,1)} %hid_h.1, bf16[16,2048,128]{2,1,0:T(8,128)(2,1)} %bitcast.7, f32[12,128]{1,0:T(8,128)} %bitcast.10, f32[12,128]{1,0:T(8,128)} %bitcast.11, f32[1,128]{1,0:T(1,128)} %constant.2.clone.freq_h, ...), custom_call_target="tpu_custom_call" | custom-call | flops 1500000000 | bytes 16000000 | tf_op jit(solution)/shard_map/layer/pallas_call | solution.py:465
  65.9 1.3 %copy.17 = bf16[16,384]{1,0:T(8,128)(2,1)} copy(bf16[16,384]{1,0:T(8,128)(2,1)} %layer.1) | data formatting | bytes 24576

commit v7 on v6

--- a/solution.py
+++ b/solution.py
@@ -116,7 +116,7 @@
     peers = [(0, tc(k)) for k in range(1, n_tp)] + [(1, tc(k)) for k in range(n_tp)]
     far_rep = lambda side: rep if side == 0 else 1 - rep
     greet = [{"rep": far_rep(side), "tp": t} for side, t in peers]
-    greet += [at(yc(k), z) for k in range(1, NY)] + [nbr[0], nbr[1]]
+    greet += [at(yc(k), z) for k in range(1, NY)] + [nbr[0], nbr[1], at(y, zc(opp))]
     for dev in greet:
         pl.semaphore_signal(barrier, inc=1, device_id=dev, device_id_type=MESH)
     pl.semaphore_wait(barrier, len(greet))
@@ -369,42 +369,36 @@
 
     def b_step(k):
         if k == opp:
-            value = b_own(zc(k)).astype(bf)
-            for d in (0, 1):
-                lanes = part_fb[d]
-                sb[d, k, :, lanes] = value[:, lanes]
-                send(sb.at[d, k, :, lanes], rb.at[d, k, :, lanes], rsb_s.at[1], rsb_r.at[d, k], nbr[d])
+            sb[0, k] = b_own(zc(k)).astype(bf)
+            send(sb.at[0, k], rb.at[0, k], rsb_s.at[1], rsb_r.at[0, k], at(y, zc(k)))
             return
         for d in (0, 1):
             value = b_own(zc(k) if d == 0 else zc(-k))
-            if k == opp - 1:
-                lanes = part_fb[d]
-                took(rb.at[d, k + 1, :, lanes], rsb_s.at[0], rsb_r.at[d, k + 1], nbr[d])
-                added = value[:, lanes] + rb[d, k + 1, :, lanes].astype(f32)
-                value = jnp.concatenate([added, value[:, part_fb[1]]] if d == 0 else [value[:, part_fb[0]], added], axis=1)
-            else:
+            if k < opp - 1:
                 took(rb.at[d, k + 1], rsb_s.at[0], rsb_r.at[d, k + 1], nbr[d])
                 value = value + rb[d, k + 1].astype(f32)
             sb[d, k] = value.astype(bf)
             send(sb.at[d, k], rb.at[d, k], rsb_s.at[0], rsb_r.at[d, k], nbr[d])
 
     a_step(4)
+    b_step(3)
     a_step(3)
+    b_step(2)
     b_step(4)
     a_step(2)
-    b_step(3)
+    b_step(1)
     a_step(1)
-    b_step(2)
     for k in AWAY:
         yb = yc(k)
         ys[yb] = (pa[z, yb] + a_took(0, 1, k) + a_took(1, 1, k)).astype(bf)
         send(ys.at[yb], yr.at[y], ry_s, ry_r, at(yb, z))
     total_a = pa[z, y] + a_took(0, 1, 0) + a_took(1, 1, 0)
-    b_step(1)
     total_b = b_own(z)
     for d in (0, 1):
         took(rb.at[d, 1], rsb_s.at[0], rsb_r.at[d, 1], nbr[d])
         total_b = total_b + rb[d, 1].astype(f32)
+    took(rb.at[0, opp], rsb_s.at[1], rsb_r.at[0, opp], at(y, zc(opp)))
+    total_b = total_b + rb[0, opp].astype(f32)
     took(yr.at[0:NY - 1], ry_s, ry_r, partner)
     for k in AWAY:
         total_a = total_a + yr[yc(k)].astype(f32)

time: 67.4 us -> 68.1 us (1.010)
  no operation moved by 1% of the time
where the time goes in v7:
time: 68.1 us; the launch traced here: 67.8 us
  Pallas kernels  65.9 us (97%)
  local copies, waits for them, and re-layouts  1.31 us (2%)
    pallas_call x1, Pallas kernels, layer(): pl.pallas_call(functools.partial(layer_kernel, n_tp, n_req), name='layer'...  65.9 us

profile of v7, /device:TPU:8, one launch (start us, length us, event | category | flops | bytes accessed | tf_op | source)
XLA Modules:
  0.0 67.8 jit_solution(13849640416071948360)
XLA Ops:
  0.7 65.9 %layer.1 = bf16[16,384]{1,0:T(8,128)(2,1)} custom-call(s32[2,16]{1,0:T(2,128)} %len_h.1, s32[1]{0:T(128)S(6)} %copy.16.mig_s, bf16[16,384]{1,0:T(8,128)(2,1)} %hid_h.1, bf16[16,2048,128]{2,1,0:T(8,128)(2,1)} %bitcast.7, f32[12,128]{1,0:T(8,128)} %bitcast.10, f32[12,128]{1,0:T(8,128)} %bitcast.11, f32[1,128]{1,0:T(1,128)} %constant.2.clone.freq_h, ...), custom_call_target="tpu_custom_call" | custom-call | flops 1500000000 | bytes 16000000 | tf_op jit(solution)/shard_map/layer/pallas_call | solution.py:459
  66.5 1.3 %copy.17 = bf16[16,384]{1,0:T(8,128)(2,1)} copy(bf16[16,384]{1,0:T(8,128)(2,1)} %layer.1) | data formatting | bytes 24576
